TPU v7x, 512 devices: a whole 4x8x8 slice. The times are simulated.
512 devices in a mesh: sec: 16 (over z_lo, x), dev: 32 (over y, z_hi, core).
Axes of the slice: x: 4, y: 8, z: 8 (z_hi: 2, z_lo: 4; z = z_hi * 4 + z_lo), core: 2. Of those that a mesh axis runs over, the one named last changes fastest.
Arguments:
- tile_inverse: bfloat16 [512, 4, 512, 512], P(('sec', 'dev'))
- link_coupling: bfloat16 [512, 512, 2048], P(('sec', 'dev')), may hold values from -0.125 to 0.125
- link_panels: int32 [512, 4], P(('sec', 'dev')), may hold values from 0 to 63, all different within a row
- leaf_rhs: bfloat16 [512, 48, 2048], P(('sec', 'dev')), may hold values from -6 to 6
- leaf_scale: float32 [512, 2048], P(('sec', 'dev')), may hold values from 0.1 to 0.5
- link_scale: float32 [8192], replicated, may hold values from 0.2 to 2
- link_inverse: bfloat16 [8192, 8192], P('sec', 'dev'), as said below
Outputs:
- leaf_step: bfloat16 [512, 48, 2048], P(('sec', 'dev'))
- link_step: bfloat16 [48, 8192], P(None, 'dev')
Inputs may be any that keep to these rules, and one draw needn't show every extreme that they name: `link_panels`: the 4 panels of one block are different. link_inverse is symmetric.
All inputs are finite; a program needn't handle non-finite values.
Results may differ from a plain program's by a relative error of at most 0.02.
Values may be sent and summed in bfloat16 or wider, within the bound.
No kernel may reach another device: no remote copies, remote signals or barrier semaphores. Data moves between devices by JAX's collectives and lax.ppermute only.
A program may use at most 64 MiB of HBM per device.

v0:
```python
import jax
import jax.numpy as jnp
from jax import lax
from jax.experimental import pallas as pl
from jax.experimental.pallas import tpu as pltpu
from jax.sharding import Mesh, PartitionSpec as P

PANEL = 128
PB = 4
SOLVES = 5
ROWS = 8
SETS = 8
PER_SET = 6
SPLIT = ("zlo", "x", "y", "zhi", "core")
Z = ("zhi", "zlo")
GROUP = ("x", "y", "core")
LINE = ("y", "core")
BF16 = jnp.bfloat16
F32 = jnp.float32
I32 = jnp.int32


def owner_of(panel):
    return ((panel >> 2) & 3) * 16 + (panel >> 4) * 4 + (panel & 3)


def place_of(panel):
    return (panel >> 3) * 8 + ((panel >> 1) & 1) * 4 + ((panel >> 2) & 1) * 2 + (panel & 1)


def dot(a, b):
    return lax.dot_general(a, b, (((1,), (0,)), ((), ())), preferred_element_type=F32)


def dot_t(a, b):
    return lax.dot_general(a, b, (((1,), (1,)), ((), ())), preferred_element_type=F32)


def iota(shape, dim):
    return lax.broadcasted_iota(I32, shape, dim)


def one_hot(condition):
    return jnp.where(condition, 1.0, 0.0)


def diagonals(starts, width, stride, rows=ROWS):
    lane, row = iota((ROWS, width), 1), iota((ROWS, width), 0)
    return jnp.concatenate(
        [one_hot((lane - row * stride == start) & (row < rows)) for start in starts], axis=0
    )


def by_tiles(tile_ref, vectors):
    tiles, size = tile_ref.shape[0], tile_ref.shape[1]
    return jnp.concatenate(
        [dot_t(vectors[:, t * size : (t + 1) * size], tile_ref[t]) for t in range(tiles)], axis=1
    ).astype(BF16)


def touched_pieces(corrected, tile_ref, coupling_ref, pack):
    solved = by_tiles(tile_ref, corrected)
    touched = dot_t(solved, coupling_ref[...]).astype(BF16)
    rows = jnp.concatenate([touched[:, s * PANEL : (s + 1) * PANEL] for s in range(PB)], axis=0)
    return dot(pack, rows)


def solve_leaf(rows, corrected_ref, tile_ref, coupling_ref):
    columns = corrected_ref.shape[0]
    picked = jnp.concatenate([rows[s * columns : (s + 1) * columns] for s in range(PB)], axis=1)
    pushed = dot(picked, coupling_ref[...])
    reduced = (corrected_ref[...].astype(F32) - pushed).astype(BF16)
    return by_tiles(tile_ref, reduced)


def unpacker(panels):
    starts = [s * ROWS + c for s in range(panels) for c in range(PER_SET)]
    return diagonals(starts, SETS * panels * ROWS, panels * ROWS).astype(BF16)


def first_kernel(panels_ref, rhs_ref, tile_ref, coupling_ref, out_ref, pack_ref, unpack_ref):
    columns = rhs_ref.shape[0]
    starts = [s * columns + zi for zi in range(SETS) for s in range(PB)]
    pack = diagonals(starts, PB * columns, SETS, PER_SET).astype(BF16)
    pack_ref[...] = pack
    unpack_ref[...] = unpacker(PB)
    pieces = touched_pieces(rhs_ref[...], tile_ref, coupling_ref, pack)
    row = iota(pieces.shape, 0)
    for s in range(PB):
        here = row % (PB * ROWS) == s * ROWS + PER_SET
        pieces = jnp.where(here, panels_ref[0, s].astype(F32), pieces)
    out_ref[...] = pieces.astype(BF16)


def first_spread_kernel(pieces_ref, out_ref, spread_ref, pick_ref):
    rows, cells = pieces_ref.shape[0], spread_ref.shape[0]
    lane, row = iota((rows, rows), 1), iota((rows, rows), 0)
    copy = one_hot((lane // ROWS == row // ROWS) & (lane % ROWS == PER_SET)).astype(BF16)
    numbers = dot(copy, pieces_ref[...])
    down = jnp.concatenate([numbers.astype(I32)] * (cells // PANEL), axis=1)
    lane, row = iota((rows, cells), 1), iota((rows, cells), 0)
    same = (lane % ROWS == row % ROWS) & (row % ROWS < PER_SET)
    pick_ref[...] = one_hot(same & (place_of(down) == lane // ROWS)).astype(BF16)
    corner = one_hot(iota((ROWS, PANEL), 1) == 0).astype(BF16)
    across = dot_t(corner, numbers.astype(BF16)).astype(I32)
    across = jnp.concatenate([owner_of(across)] * (cells // ROWS), axis=0)
    lane, row = iota((cells, rows), 1), iota((cells, rows), 0)
    same = (lane % ROWS == row % ROWS) & (row % ROWS < PER_SET)
    spread = one_hot(same & (across == row // ROWS)).astype(BF16)
    spread_ref[...] = spread
    out_ref[...] = dot(spread, pieces_ref[...]).astype(BF16)


def select_kernel(select_ref, pieces_ref, out_ref):
    out_ref[...] = dot(select_ref[...], pieces_ref[...]).astype(BF16)


def sum_of(pieces_ref):
    total = pieces_ref[0].astype(F32)
    for m in range(1, pieces_ref.shape[0]):
        total = total + pieces_ref[m].astype(F32)
    return total


def copies(out_ref, value):
    for m in range(out_ref.shape[0]):
        out_ref[m] = value


def first_rhs_kernel(pieces_ref, out_ref):
    copies(out_ref, (-sum_of(pieces_ref)).astype(BF16))


def rhs_kernel(where_ref, pieces_ref, step_ref, scale_ref, out_ref):
    step = step_ref[where_ref[1]].astype(F32)
    side = -scale_ref[pl.ds(where_ref[0], 1), :] * step
    copies(out_ref, (side - sum_of(pieces_ref)).astype(BF16))


def step_kernel(pieces_ref, inverse_ref, out_ref):
    rhs = jnp.concatenate([pieces_ref[m] for m in range(pieces_ref.shape[0])], axis=1)
    parts = [dot(rhs, inverse_ref[zh]) for zh in range(2)]
    parts = [part[:, h * PANEL : (h + 1) * PANEL] for part in parts for h in range(2)]
    copies(out_ref, jnp.concatenate(parts, axis=0).astype(BF16))


def total_kernel(pieces_ref, out_ref):
    copies(out_ref, sum_of(pieces_ref).astype(BF16))


def last_total_kernel(pieces_ref, out_ref, own_ref):
    total = sum_of(pieces_ref).astype(BF16)
    copies(out_ref, total)
    own_ref[...] = total


def last_pick_kernel(select_ref, pieces_ref, own_ref, out_ref):
    picked = dot(select_ref[...], pieces_ref[...]).astype(BF16)
    size = picked.shape[0] // SETS
    for zi in range(SETS):
        half = (zi // 4) * 2 * ROWS
        out_ref[zi, :size] = picked[zi * size : (zi + 1) * size]
        out_ref[zi, size:] = own_ref[half : half + 2 * ROWS]


def middle_kernel(
    pieces_ref, unpack_ref, pack_ref, corrected_ref, rhs_ref, scale_ref, tile_ref, coupling_ref,
    out_ref, next_ref,
):
    rows = dot(unpack_ref[...], pieces_ref[...]).astype(BF16)
    leaf = solve_leaf(rows, corrected_ref, tile_ref, coupling_ref)
    corrected = (rhs_ref[...].astype(F32) - scale_ref[...] * leaf.astype(F32)).astype(BF16)
    next_ref[...] = corrected
    out_ref[...] = touched_pieces(corrected, tile_ref, coupling_ref, pack_ref[...]).astype(BF16)


def last_kernel(
    pieces_ref, unpack_ref, corrected_ref, tile_ref, coupling_ref, leaf_ref, link_ref
):
    columns = corrected_ref.shape[0]
    size = PB * ROWS
    pieces = jnp.concatenate([pieces_ref[zi, :size] for zi in range(SETS)], axis=0)
    rows = dot(unpack_ref[...], pieces).astype(BF16)
    leaf_ref[...] = solve_leaf(rows, corrected_ref, tile_ref, coupling_ref)
    link = jnp.concatenate([pieces_ref[zi, size:] for zi in range(SETS)], axis=0)
    link = dot(unpacker(2), link).astype(BF16)
    link_ref[...] = jnp.concatenate([link[:columns], link[columns:]], axis=1)


INTERPRET = False


def call(body, name, shapes, *operands):
    outs = [jax.ShapeDtypeStruct(s, BF16) for s in shapes]
    vmem, smem = (pl.BlockSpec(memory_space=s) for s in (pltpu.VMEM, pltpu.SMEM))
    return pl.pallas_call(
        body,
        name=name,
        out_shape=outs,
        in_specs=[smem if x.dtype == I32 else vmem for x in operands],
        out_specs=[vmem] * len(outs),
        compiler_params=pltpu.CompilerParams(vmem_limit_bytes=24 << 20),
        interpret=INTERPRET,
    )(*operands)


def swap(x, axes):
    return lax.all_to_all(x, axes, 0, 0, tiled=True)


def per_device(
    tile_inverse, link_coupling, link_panels, leaf_rhs, leaf_scale, link_scale, link_inverse
):
    tile_inv, coupling, own_rhs = tile_inverse[0], link_coupling[0], leaf_rhs[0]
    columns = own_rhs.shape[0]
    assert columns == SETS * PER_SET
    x, y, core = lax.axis_index("x"), lax.axis_index("y"), lax.axis_index("core")
    line, members = lax.axis_size(LINE), lax.axis_size(GROUP)

    with jax.named_scope("gather"):
        inverse = lax.all_gather(link_inverse, Z)
        inverse = inverse.reshape(2, -1, link_inverse.shape[1])
    scales = link_scale.reshape(-1, PANEL)
    place = y * 2 + core
    panel = (place >> 2) * 16 + x * 4 + (place & 3)
    where = jnp.stack([panel, place_of(panel)]).astype(I32)

    home = (SETS * PB * ROWS, PANEL)
    flat = (members * ROWS, PANEL)
    mixer = (PB * columns, SETS * PB * ROWS)
    parts = (4 * ROWS, PANEL)
    corrected = own_rhs
    pieces, pack, unpack = call(
        first_kernel, "first", [home, mixer[::-1], mixer], link_panels, own_rhs, tile_inv, coupling
    )
    for solve_index in range(SOLVES):
        last = solve_index == SOLVES - 1
        pieces = swap(pieces.reshape(SETS, PB * ROWS, PANEL), Z).reshape(home)
        if solve_index == 0:
            pieces, spread, pick = call(
                first_spread_kernel, "spread", [flat, (flat[0], home[0]), (home[0], flat[0])], pieces
            )
        else:
            pieces, = call(select_kernel, "spread", [flat], spread, pieces)
        pieces = swap(pieces.reshape(members, ROWS, PANEL), GROUP)
        if solve_index == 0:
            pieces, = call(first_rhs_kernel, "rhs", [(line, ROWS, PANEL)], pieces)
        else:
            pieces, = call(rhs_kernel, "rhs", [(line, ROWS, PANEL)], where, pieces, step, scales)
        pieces = swap(pieces, LINE)
        pieces, = call(step_kernel, "step", [(4,) + parts], pieces, inverse)
        pieces = swap(pieces, "x")
        if last:
            pieces, own = call(last_total_kernel, "total", [(line,) + parts, parts], pieces)
        else:
            pieces, = call(total_kernel, "total", [(line,) + parts], pieces)
        pieces = swap(pieces, LINE)
        step, pieces = pieces.reshape(members, ROWS, PANEL), pieces.reshape(flat)
        if last:
            wide = (SETS, (PB + 2) * ROWS, PANEL)
            pieces, = call(last_pick_kernel, "pick", [wide], pick, pieces, own)
            leaf, link = call(
                last_kernel, "last", [own_rhs.shape, (columns, 2 * PANEL)],
                swap(pieces, Z), unpack, corrected, tile_inv, coupling,
            )
        else:
            pieces, = call(select_kernel, "pick", [home], pick, pieces)
            pieces = swap(pieces.reshape(SETS, PB * ROWS, PANEL), Z).reshape(home)
            pieces, corrected = call(
                middle_kernel, "middle", [home, own_rhs.shape],
                pieces, unpack, pack, corrected, own_rhs, leaf_scale, tile_inv, coupling,
            )
    return leaf[None], link


def solution(mesh):
    fine = Mesh(mesh.devices.reshape(4, 4, 8, 2, 2), SPLIT)
    sec, dev = SPLIT[:2], SPLIT[2:]
    in_specs = (
        P(SPLIT, None, None, None),
        P(SPLIT, None, None),
        P(SPLIT, None),
        P(SPLIT, None, None),
        P(SPLIT, None),
        P(),
        P(sec, dev),
    )
    out_specs = (P(SPLIT, None, None), P(None, dev))
    return jax.shard_map(
        per_device, mesh=fine, in_specs=in_specs, out_specs=out_specs, check_vma=False
    )
```

profile of v0, /device:TPU:1, one launch (start us, length us, event | category | flops | bytes accessed | tf_op | source)
XLA Modules:
  0.0 394.0 jit_solution(9858176132577287705)
XLA Ops:
  14.8 18.0 %all_to_all.150 = bf16[8,32,128]{2,1,0:T(8,128)(2,1)S(1)} all-to-all(bf16[8,32,128]{2,1,0:T(8,128)(2,1)S(1)} %bitcast.96), channel_id=1, replica_groups=mesh['zlo'=4,'x'=4,'y'=8,'zhi'=2,'core'=2] {'zhi','zlo'}, dimensions={0} | all-to-all | bytes 131072 | tf_op jit(solution)/shard_map/all_to_all | solution.py:208
  33.3 22.5 %all_to_all.151.pieces_ref = bf16[64,8,128]{2,1,0:T(8,128)(2,1)S(1)} all-to-all(bf16[64,8,128]{2,1,0:T(8,128)(2,1)S(1)} %bitcast.92), channel_id=1, replica_groups=mesh['zlo'=4,'x'=4,'y'=8,'zhi'=2,'core'=2] {'x','y','core'}, dimensions={0} | all-to-all | bytes 262144 | tf_op jit(solution)/shard_map/all_to_all | solution.py:208
  55.9 10.6 %all_to_all.152.pieces_ref = bf16[16,8,128]{2,1,0:T(8,128)(2,1)S(1)} all-to-all(bf16[16,8,128]{2,1,0:T(8,128)(2,1)S(1)} %rhs.5), channel_id=1, replica_groups=mesh['zlo'=4,'x'=4,'y'=8,'zhi'=2,'core'=2] {'y','core'}, dimensions={0} | all-to-all | bytes 65536 | tf_op jit(solution)/shard_map/all_to_all | solution.py:208
  75.2 13.3 %all_to_all.154 = bf16[16,32,128]{2,1,0:T(8,128)(2,1)S(1)} all-to-all(bf16[16,32,128]{2,1,0:T(8,128)(2,1)S(1)} %total.5), channel_id=1, replica_groups=mesh['zlo'=4,'x'=4,'y'=8,'zhi'=2,'core'=2] {'y','core'}, dimensions={0} | all-to-all | bytes 262144 | tf_op jit(solution)/shard_map/all_to_all | solution.py:208
  88.7 9.7 %all_to_all.155 = bf16[8,32,128]{2,1,0:T(8,128)(2,1)S(1)} all-to-all(bf16[8,32,128]{2,1,0:T(8,128)(2,1)S(1)} %bitcast.87), channel_id=1, replica_groups=mesh['zlo'=4,'x'=4,'y'=8,'zhi'=2,'core'=2] {'zhi','zlo'}, dimensions={0} | all-to-all | bytes 131072 | tf_op jit(solution)/shard_map/all_to_all | solution.py:208
  102.5 9.6 %all_to_all.156 = bf16[8,32,128]{2,1,0:T(8,128)(2,1)S(1)} all-to-all(bf16[8,32,128]{2,1,0:T(8,128)(2,1)S(1)} %bitcast.97), channel_id=1, replica_groups=mesh['zlo'=4,'x'=4,'y'=8,'zhi'=2,'core'=2] {'zhi','zlo'}, dimensions={0} | all-to-all | bytes 131072 | tf_op jit(solution)/shard_map/all_to_all | solution.py:208
  119.8 10.3 %all-to-all-done.7.pieces_ref = bf16[64,8,128]{2,1,0:T(8,128)(2,1)S(1)} async-done(((bf16[64,8,128]{2,1,0:T(8,128)(2,1)}), bf16[64,8,128]{2,1,0:T(8,128)(2,1)S(1)}, u32[]{:S(2)}, u32[]{:S(2)}) %all-to-all-start.7) | async-done | bytes 131104 | tf_op jit(solution)/shard_map/all_to_all | solution.py:208
  130.8 10.8 %all_to_all.157.pieces_ref = bf16[16,8,128]{2,1,0:T(8,128)(2,1)S(1)} all-to-all(bf16[16,8,128]{2,1,0:T(8,128)(2,1)S(1)} %rhs.6), channel_id=1, replica_groups=mesh['zlo'=4,'x'=4,'y'=8,'zhi'=2,'core'=2] {'y','core'}, dimensions={0} | all-to-all | bytes 65536 | tf_op jit(solution)/shard_map/all_to_all | solution.py:208
  150.2 13.3 %all_to_all.159 = bf16[16,32,128]{2,1,0:T(8,128)(2,1)S(1)} all-to-all(bf16[16,32,128]{2,1,0:T(8,128)(2,1)S(1)} %total.6), channel_id=1, replica_groups=mesh['zlo'=4,'x'=4,'y'=8,'zhi'=2,'core'=2] {'y','core'}, dimensions={0} | all-to-all | bytes 262144 | tf_op jit(solution)/shard_map/all_to_all | solution.py:208
  163.7 10.5 %all_to_all.160 = bf16[8,32,128]{2,1,0:T(8,128)(2,1)S(1)} all-to-all(bf16[8,32,128]{2,1,0:T(8,128)(2,1)S(1)} %bitcast.88), channel_id=1, replica_groups=mesh['zlo'=4,'x'=4,'y'=8,'zhi'=2,'core'=2] {'zhi','zlo'}, dimensions={0} | all-to-all | bytes 131072 | tf_op jit(solution)/shard_map/all_to_all | solution.py:208
  186.7 15.3 %all_to_all.162.pieces_ref = bf16[64,8,128]{2,1,0:T(8,128)(2,1)S(1)} all-to-all(bf16[64,8,128]{2,1,0:T(8,128)(2,1)S(1)} %bitcast.76), channel_id=1, replica_groups=mesh['zlo'=4,'x'=4,'y'=8,'zhi'=2,'core'=2] {'x','y','core'}, dimensions={0} | all-to-all | bytes 262144 | tf_op jit(solution)/shard_map/all_to_all | solution.py:208
  202.6 10.6 %all_to_all.163.pieces_ref = bf16[16,8,128]{2,1,0:T(8,128)(2,1)S(1)} all-to-all(bf16[16,8,128]{2,1,0:T(8,128)(2,1)S(1)} %rhs.7), channel_id=1, replica_groups=mesh['zlo'=4,'x'=4,'y'=8,'zhi'=2,'core'=2] {'y','core'}, dimensions={0} | all-to-all | bytes 65536 | tf_op jit(solution)/shard_map/all_to_all | solution.py:208
  220.3 13.3 %all_to_all.165 = bf16[16,32,128]{2,1,0:T(8,128)(2,1)S(1)} all-to-all(bf16[16,32,128]{2,1,0:T(8,128)(2,1)S(1)} %total.7), channel_id=1, replica_groups=mesh['zlo'=4,'x'=4,'y'=8,'zhi'=2,'core'=2] {'y','core'}, dimensions={0} | all-to-all | bytes 262144 | tf_op jit(solution)/shard_map/all_to_all | solution.py:208
  233.8 10.5 %all_to_all.166 = bf16[8,32,128]{2,1,0:T(8,128)(2,1)S(1)} all-to-all(bf16[8,32,128]{2,1,0:T(8,128)(2,1)S(1)} %bitcast.89), channel_id=1, replica_groups=mesh['zlo'=4,'x'=4,'y'=8,'zhi'=2,'core'=2] {'zhi','zlo'}, dimensions={0} | all-to-all | bytes 131072 | tf_op jit(solution)/shard_map/all_to_all | solution.py:208
  247.0 9.6 %all_to_all.167 = bf16[8,32,128]{2,1,0:T(8,128)(2,1)S(1)} all-to-all(bf16[8,32,128]{2,1,0:T(8,128)(2,1)S(1)} %bitcast.95), channel_id=1, replica_groups=mesh['zlo'=4,'x'=4,'y'=8,'zhi'=2,'core'=2] {'zhi','zlo'}, dimensions={0} | all-to-all | bytes 131072 | tf_op jit(solution)/shard_map/all_to_all | solution.py:208
  256.8 15.3 %all_to_all.168.pieces_ref = bf16[64,8,128]{2,1,0:T(8,128)(2,1)S(1)} all-to-all(bf16[64,8,128]{2,1,0:T(8,128)(2,1)S(1)} %bitcast.77), channel_id=1, replica_groups=mesh['zlo'=4,'x'=4,'y'=8,'zhi'=2,'core'=2] {'x','y','core'}, dimensions={0} | all-to-all | bytes 262144 | tf_op jit(solution)/shard_map/all_to_all | solution.py:208
  272.7 10.6 %all_to_all.169.pieces_ref = bf16[16,8,128]{2,1,0:T(8,128)(2,1)S(1)} all-to-all(bf16[16,8,128]{2,1,0:T(8,128)(2,1)S(1)} %rhs.8), channel_id=1, replica_groups=mesh['zlo'=4,'x'=4,'y'=8,'zhi'=2,'core'=2] {'y','core'}, dimensions={0} | all-to-all | bytes 65536 | tf_op jit(solution)/shard_map/all_to_all | solution.py:208
  290.4 13.3 %all_to_all.171 = bf16[16,32,128]{2,1,0:T(8,128)(2,1)S(1)} all-to-all(bf16[16,32,128]{2,1,0:T(8,128)(2,1)S(1)} %total.8), channel_id=1, replica_groups=mesh['zlo'=4,'x'=4,'y'=8,'zhi'=2,'core'=2] {'y','core'}, dimensions={0} | all-to-all | bytes 262144 | tf_op jit(solution)/shard_map/all_to_all | solution.py:208
  303.9 10.5 %all_to_all.172 = bf16[8,32,128]{2,1,0:T(8,128)(2,1)S(1)} all-to-all(bf16[8,32,128]{2,1,0:T(8,128)(2,1)S(1)} %bitcast.90), channel_id=1, replica_groups=mesh['zlo'=4,'x'=4,'y'=8,'zhi'=2,'core'=2] {'zhi','zlo'}, dimensions={0} | all-to-all | bytes 131072 | tf_op jit(solution)/shard_map/all_to_all | solution.py:208
  317.1 9.6 %all_to_all.173 = bf16[8,32,128]{2,1,0:T(8,128)(2,1)S(1)} all-to-all(bf16[8,32,128]{2,1,0:T(8,128)(2,1)S(1)} %bitcast.93), channel_id=1, replica_groups=mesh['zlo'=4,'x'=4,'y'=8,'zhi'=2,'core'=2] {'zhi','zlo'}, dimensions={0} | all-to-all | bytes 131072 | tf_op jit(solution)/shard_map/all_to_all | solution.py:208
  326.9 15.3 %all_to_all.174.pieces_ref = bf16[64,8,128]{2,1,0:T(8,128)(2,1)S(1)} all-to-all(bf16[64,8,128]{2,1,0:T(8,128)(2,1)S(1)} %bitcast.75), channel_id=1, replica_groups=mesh['zlo'=4,'x'=4,'y'=8,'zhi'=2,'core'=2] {'x','y','core'}, dimensions={0} | all-to-all | bytes 262144 | tf_op jit(solution)/shard_map/all_to_all | solution.py:208
  342.8 10.6 %all_to_all.175.pieces_ref = bf16[16,8,128]{2,1,0:T(8,128)(2,1)S(1)} all-to-all(bf16[16,8,128]{2,1,0:T(8,128)(2,1)S(1)} %rhs.9), channel_id=1, replica_groups=mesh['zlo'=4,'x'=4,'y'=8,'zhi'=2,'core'=2] {'y','core'}, dimensions={0} | all-to-all | bytes 65536 | tf_op jit(solution)/shard_map/all_to_all | solution.py:208
  360.5 13.3 %all_to_all.177 = bf16[16,32,128]{2,1,0:T(8,128)(2,1)S(1)} all-to-all(bf16[16,32,128]{2,1,0:T(8,128)(2,1)S(1)} %get-tuple-element.33), channel_id=1, replica_groups=mesh['zlo'=4,'x'=4,'y'=8,'zhi'=2,'core'=2] {'y','core'}, dimensions={0} | all-to-all | bytes 262144 | tf_op jit(solution)/shard_map/all_to_all | solution.py:208
  374.0 11.2 %all_to_all.178.pieces_ref = bf16[8,48,128]{2,1,0:T(8,128)(2,1)S(1)} all-to-all(bf16[8,48,128]{2,1,0:T(8,128)(2,1)S(1)} %pick.9), channel_id=1, replica_groups=mesh['zlo'=4,'x'=4,'y'=8,'zhi'=2,'core'=2] {'zhi','zlo'}, dimensions={0} | all-to-all | bytes 196608 | tf_op jit(solution)/shard_map/all_to_all | solution.py:208
  (68 shorter events, 82.0 us)
Async XLA Ops:
  7.2 59.3 %all-gather.3.cloned.1.call-start = ((), (), s32[]{:S(2)}) async-start(), calls=%async_computation.30 | async-start | bytes 2359296 | tf_op jit(solution)/shard_map/gather/all_gather | solution.py:221
  7.9 1.6 copy-start
  9.5 1.6 copy-start.2
  11.1 0.9 copy-start.8
  12.0 0.7 copy-start.12
  12.7 85.6 %copy-start.9 = (bf16[1,48,2048]{2,1,0:T(8,128)(2,1)S(1)}, bf16[1,48,2048]{2,1,0:T(8,128)(2,1)}, u32[]{:S(2)}) copy-start(bf16[1,48,2048]{2,1,0:T(8,128)(2,1)} %param.10) | copy-start | bytes 589828
  12.7 85.6 %copy-start.11 = (f32[1,2048]{1,0:T(1,128)S(1)}, f32[1,2048]{1,0:T(1,128)}, u32[]{:S(2)}) copy-start(f32[1,2048]{1,0:T(1,128)} %scale_ref.7) | copy-start | bytes 24580
  14.7 83.6 %copy-start.1 = (bf16[1,4,512,512]{3,2,1,0:T(8,128)(2,1)S(1)}, bf16[1,4,512,512]{3,2,1,0:T(8,128)(2,1)}, u32[]{:S(2)}) copy-start(bf16[1,4,512,512]{3,2,1,0:T(8,128)(2,1)} %param.7) | copy-start | bytes 6291460
  66.5 1.6 copy-start.5
  98.3 1.6 copy-start.3
  99.9 30.3 %copy-start.10 = (f32[8192]{0:T(1024)S(1)}, f32[8192]{0:T(1024)}, u32[]{:S(2)}) copy-start(f32[8192]{0:T(1024)} %param.12) | copy-start | bytes 98308
  113.0 17.1 %all-to-all-start.7 = ((bf16[64,8,128]{2,1,0:T(8,128)(2,1)}), bf16[64,8,128]{2,1,0:T(8,128)(2,1)S(1)}, u32[]{:S(2)}, u32[]{:S(2)}) async-start(bf16[64,8,128]{2,1,0:T(8,128)(2,1)} %bitcast.14), calls=%async_computation.7 | async-start | bytes 262144 | tf_op jit(solution)/shard_map/all_to_all | solution.py:208
  130.2 44.1 %copy-start.4 = (bf16[1,512,2048]{2,1,0:T(8,128)(2,1)S(1)}, bf16[1,512,2048]{2,1,0:T(8,128)(2,1)}, u32[]{:S(2)}) copy-start(bf16[1,512,2048]{2,1,0:T(8,128)(2,1)} %param.8) | copy-start | bytes 6291460
  141.6 1.6 copy-start.6
  174.2 39.0 %copy-start.7 = (bf16[4096,256]{1,0:T(8,128)(2,1)S(1)}, bf16[4096,256]{1,0:T(8,128)(2,1)}, u32[]{:S(2)}) copy-start(bf16[4096,256]{1,0:T(8,128)(2,1)} %all-gather.3.cloned.1.call-done) | copy-start | bytes 6291460
Sparse Core Ops, SparseCore 0:
  10.1 45.3 all-gather.2
where the time goes:
time: 395 us; the launch traced here: 394 us
  blocking collectives  330 us (84%)
  Pallas kernels  22.1 us (6%)
  between operations  14.2 us (4%)
  waiting for transfers between devices  11 us (3%)
  local copies, waits for them, and re-layouts  9.55 us (2%)
  starting transfers between devices  6.74 us (2%)
    all_to_all x29, blocking collectives, swap(): return lax.all_to_all(x, axes, 0, 0, tiled=True)  330 us
    pallas_call x31, Pallas kernels, call(): pl.pallas_call(body, name=name, out_shape=outs, in_specs=[smem if x.dtype...  22.1 us
    all_to_all x1, waiting for transfers between devices, swap(): return lax.all_to_all(x, axes, 0, 0, tiled=True)  10.3 us
    unnamed x26, local copies, waits for them, and re-layouts  9.55 us
  transfers between devices with their start and end apart: 2, of which 1 were waited for; matrix products, arithmetic and copies ran while one was open for 0% of the time, Pallas kernels for 1%

commit v1 on v0

--- a/solution.py
+++ b/solution.py
@@ -4,6 +4,7 @@
 from jax.experimental import pallas as pl
 from jax.experimental.pallas import tpu as pltpu
 from jax.sharding import Mesh, PartitionSpec as P
+
 
 PANEL = 128
 PB = 4
@@ -78,12 +79,24 @@
     return diagonals(starts, SETS * panels * ROWS, panels * ROWS).astype(BF16)
 
 
-def first_kernel(panels_ref, rhs_ref, tile_ref, coupling_ref, out_ref, pack_ref, unpack_ref):
+def first_kernel(
+    panels_ref, rhs_hbm, tile_hbm, coupling_hbm, out_ref, pack_ref, unpack_ref,
+    rhs_ref, tile_ref, coupling_ref, sems,
+):
     columns = rhs_ref.shape[0]
+    fetches = [
+        pltpu.make_async_copy(rhs_hbm, rhs_ref, sems.at[0]),
+        pltpu.make_async_copy(tile_hbm, tile_ref, sems.at[1]),
+        pltpu.make_async_copy(coupling_hbm, coupling_ref, sems.at[2]),
+    ]
+    for fetch in fetches:
+        fetch.start()
     starts = [s * columns + zi for zi in range(SETS) for s in range(PB)]
     pack = diagonals(starts, PB * columns, SETS, PER_SET).astype(BF16)
     pack_ref[...] = pack
     unpack_ref[...] = unpacker(PB)
+    for fetch in fetches:
+        fetch.wait()
     pieces = touched_pieces(rhs_ref[...], tile_ref, coupling_ref, pack)
     row = iota(pieces.shape, 0)
     for s in range(PB):
@@ -163,15 +176,76 @@
         out_ref[zi, size:] = own_ref[half : half + 2 * ROWS]
 
 
+def correct(rhs_ref, scale_ref, leaf):
+    return (rhs_ref[...].astype(F32) - scale_ref[...] * leaf.astype(F32)).astype(BF16)
+
+
+def ahead_pieces(corrected, rhs_ref, scale_ref, tile_ref, coupling_ref, pack):
+    leaf = by_tiles(tile_ref, corrected)
+    return touched_pieces(correct(rhs_ref, scale_ref, leaf), tile_ref, coupling_ref, pack)
+
+
+def response_kernel(after_ref, scale_ref, tile_ref, coupling_ref, out_ref):
+    leaf = by_tiles(tile_ref, coupling_ref[...])
+    moved = (scale_ref[...] * leaf.astype(F32)).astype(BF16)
+    solved = by_tiles(tile_ref, moved)
+    out_ref[...] = dot_t(solved, coupling_ref[...]).astype(BF16)
+
+
 def middle_kernel(
     pieces_ref, unpack_ref, pack_ref, corrected_ref, rhs_ref, scale_ref, tile_ref, coupling_ref,
     out_ref, next_ref,
 ):
     rows = dot(unpack_ref[...], pieces_ref[...]).astype(BF16)
     leaf = solve_leaf(rows, corrected_ref, tile_ref, coupling_ref)
-    corrected = (rhs_ref[...].astype(F32) - scale_ref[...] * leaf.astype(F32)).astype(BF16)
+    corrected = correct(rhs_ref, scale_ref, leaf)
     next_ref[...] = corrected
     out_ref[...] = touched_pieces(corrected, tile_ref, coupling_ref, pack_ref[...]).astype(BF16)
+
+
+def ahead_kernel(
+    pack_ref, corrected_ref, rhs_ref, scale_ref, tile_ref, coupling_ref, out_ref
+):
+    out_ref[...] = ahead_pieces(
+        corrected_ref[...], rhs_ref, scale_ref, tile_ref, coupling_ref, pack_ref[...]
+    ).astype(BF16)
+
+
+def home_kernel(
+    pieces_ref, unpack_ref, corrected_ref, rhs_ref, scale_ref, tile_ref, coupling_ref, next_ref
+):
+    size = PB * ROWS
+    pieces = jnp.concatenate([pieces_ref[zi, :size] for zi in range(SETS)], axis=0)
+    rows = dot(unpack_ref[...], pieces).astype(BF16)
+    leaf = solve_leaf(rows, corrected_ref, tile_ref, coupling_ref)
+    next_ref[...] = correct(rhs_ref, scale_ref, leaf)
+
+
+def both_pick_kernel(select_ref, pieces_ref, ahead_ref, out_ref, picked_ref):
+    picked = dot(select_ref[...], pieces_ref[...]).astype(BF16)
+    picked_ref[...] = picked
+    size = PB * ROWS
+    for zi in range(SETS):
+        out_ref[zi, :size] = picked[zi * size : (zi + 1) * size]
+        out_ref[zi, size:] = ahead_ref[zi * size : (zi + 1) * size]
+
+
+def respond_kernel(pieces_ref, picked_ref, spread_ref, response_hbm, out_ref, response_ref, sems):
+    size, rows = PB * ROWS, []
+    fetches = [
+        pltpu.make_async_copy(response_hbm.at[zi], response_ref.at[zi], sems.at[zi])
+        for zi in range(SETS)
+    ]
+    for fetch in fetches:
+        fetch.start()
+    for zi in range(SETS):
+        places = [slice(s * ROWS, (s + 1) * ROWS) for s in range(PB)]
+        picked = jnp.concatenate([picked_ref[zi * size + p.start : zi * size + p.stop] for p in places], axis=1)
+        fetches[zi].wait()
+        added = dot(picked, response_ref[zi])
+        added = jnp.concatenate([added[:, s * PANEL : (s + 1) * PANEL] for s in range(PB)], axis=0)
+        rows.append((pieces_ref[zi, size:].astype(F32) + added).astype(BF16))
+    out_ref[...] = dot(spread_ref[...], jnp.concatenate(rows, axis=0)).astype(BF16)
 
 
 def last_kernel(
@@ -190,15 +264,27 @@
 INTERPRET = False
 
 
-def call(body, name, shapes, *operands):
+def call(body, shapes, *operands, fetched=()):
     outs = [jax.ShapeDtypeStruct(s, BF16) for s in shapes]
-    vmem, smem = (pl.BlockSpec(memory_space=s) for s in (pltpu.VMEM, pltpu.SMEM))
+    vmem, smem, anywhere = (
+        pl.BlockSpec(memory_space=s) for s in (pltpu.VMEM, pltpu.SMEM, pltpu.HBM)
+    )
+    operands = [
+        pltpu.with_memory_space_constraint(x, pltpu.HBM) if i in fetched and not INTERPRET else x
+        for i, x in enumerate(operands)
+    ]
+    scratch = [pltpu.VMEM(operands[i].shape, BF16) for i in fetched]
+    if fetched:
+        scratch.append(pltpu.SemaphoreType.DMA((SETS,)))
     return pl.pallas_call(
         body,
-        name=name,
         out_shape=outs,
-        in_specs=[smem if x.dtype == I32 else vmem for x in operands],
+        in_specs=[
+            anywhere if i in fetched else smem if x.dtype == I32 else vmem
+            for i, x in enumerate(operands)
+        ],
         out_specs=[vmem] * len(outs),
+        scratch_shapes=scratch,
         compiler_params=pltpu.CompilerParams(vmem_limit_bytes=24 << 20),
         interpret=INTERPRET,
     )(*operands)
@@ -217,9 +303,8 @@
     x, y, core = lax.axis_index("x"), lax.axis_index("y"), lax.axis_index("core")
     line, members = lax.axis_size(LINE), lax.axis_size(GROUP)
 
-    with jax.named_scope("gather"):
-        inverse = lax.all_gather(link_inverse, Z)
-        inverse = inverse.reshape(2, -1, link_inverse.shape[1])
+    inverse = lax.all_gather(link_inverse, Z)
+    inverse = inverse.reshape(2, -1, link_inverse.shape[1])
     scales = link_scale.reshape(-1, PANEL)
     place = y * 2 + core
     panel = (place >> 2) * 16 + x * 4 + (place & 3)
@@ -231,44 +316,65 @@
     parts = (4 * ROWS, PANEL)
     corrected = own_rhs
     pieces, pack, unpack = call(
-        first_kernel, "first", [home, mixer[::-1], mixer], link_panels, own_rhs, tile_inv, coupling
+        first_kernel, [home, mixer[::-1], mixer], link_panels, own_rhs, tile_inv, coupling,
+        fetched=(1, 2, 3),
     )
     for solve_index in range(SOLVES):
         last = solve_index == SOLVES - 1
-        pieces = swap(pieces.reshape(SETS, PB * ROWS, PANEL), Z).reshape(home)
+        if solve_index < 2:
+            pieces = swap(pieces.reshape(SETS, PB * ROWS, PANEL), Z).reshape(home)
         if solve_index == 0:
             pieces, spread, pick = call(
-                first_spread_kernel, "spread", [flat, (flat[0], home[0]), (home[0], flat[0])], pieces
-            )
+                first_spread_kernel, [flat, (flat[0], home[0]), (home[0], flat[0])], pieces
+            )
+            response, = call(
+                response_kernel, [(PB * PANEL,) * 2],
+                pieces, leaf_scale, tile_inv, coupling,
+            )
+            response = lax.all_gather(response, Z)
+        elif solve_index == 1:
+            pieces, = call(select_kernel, [flat], spread, pieces)
         else:
-            pieces, = call(select_kernel, "spread", [flat], spread, pieces)
+            pieces, = call(respond_kernel, [flat], both, picked, spread, response, fetched=(3,))
         pieces = swap(pieces.reshape(members, ROWS, PANEL), GROUP)
         if solve_index == 0:
-            pieces, = call(first_rhs_kernel, "rhs", [(line, ROWS, PANEL)], pieces)
+            pieces, = call(first_rhs_kernel, [(line, ROWS, PANEL)], pieces)
         else:
-            pieces, = call(rhs_kernel, "rhs", [(line, ROWS, PANEL)], where, pieces, step, scales)
+            pieces, = call(rhs_kernel, [(line, ROWS, PANEL)], where, pieces, step, scales)
         pieces = swap(pieces, LINE)
-        pieces, = call(step_kernel, "step", [(4,) + parts], pieces, inverse)
+        pieces, = call(step_kernel, [(4,) + parts], pieces, inverse)
         pieces = swap(pieces, "x")
         if last:
-            pieces, own = call(last_total_kernel, "total", [(line,) + parts, parts], pieces)
+            pieces, own = call(last_total_kernel, [(line,) + parts, parts], pieces)
         else:
-            pieces, = call(total_kernel, "total", [(line,) + parts], pieces)
+            pieces, = call(total_kernel, [(line,) + parts], pieces)
         pieces = swap(pieces, LINE)
         step, pieces = pieces.reshape(members, ROWS, PANEL), pieces.reshape(flat)
         if last:
             wide = (SETS, (PB + 2) * ROWS, PANEL)
-            pieces, = call(last_pick_kernel, "pick", [wide], pick, pieces, own)
+            pieces, = call(last_pick_kernel, [wide], pick, pieces, own)
             leaf, link = call(
-                last_kernel, "last", [own_rhs.shape, (columns, 2 * PANEL)],
+                last_kernel, [own_rhs.shape, (columns, 2 * PANEL)],
                 swap(pieces, Z), unpack, corrected, tile_inv, coupling,
             )
-        else:
-            pieces, = call(select_kernel, "pick", [home], pick, pieces)
+        elif solve_index == 0:
+            pieces, = call(select_kernel, [home], pick, pieces)
             pieces = swap(pieces.reshape(SETS, PB * ROWS, PANEL), Z).reshape(home)
             pieces, corrected = call(
-                middle_kernel, "middle", [home, own_rhs.shape],
+                middle_kernel, [home, own_rhs.shape],
                 pieces, unpack, pack, corrected, own_rhs, leaf_scale, tile_inv, coupling,
+            )
+        else:
+            both = (SETS, 2 * PB * ROWS, PANEL)
+            ahead, = call(
+                ahead_kernel, [home],
+                pack, corrected, own_rhs, leaf_scale, tile_inv, coupling,
+            )
+            both, picked = call(both_pick_kernel, [both, home], pick, pieces, ahead)
+            both = swap(both, Z)
+            corrected, = call(
+                home_kernel, [own_rhs.shape],
+                both, unpack, corrected, own_rhs, leaf_scale, tile_inv, coupling,
             )
     return leaf[None], link
 

time: 395 us -> 385 us (0.975)
  blocking collectives: 330 us -> 256 us
  Pallas kernels: 22.1 us -> 43.1 us
  waiting for transfers between devices: 11 us -> 29.3 us
  starting transfers between devices: 6.74 us -> 25 us
  local copies, waits for them, and re-layouts: 9.55 us -> 15.2 us
    all_to_all x29 -> x22, blocking collectives: 330 us -> 256 us  [swap(): return lax.all_to_all(x, axes, 0, 0, tiled=True)]
    pallas_call x31 -> x35, Pallas kernels: 22.1 us -> 43.1 us  [call(): pl.pallas_call(body, out_shape=outs, in_specs=[anywhere if i in fetched e...]
    all_to_all x1 -> x5, waiting for transfers between devices: 10.3 us -> 28.5 us  [swap(): return lax.all_to_all(x, axes, 0, 0, tiled=True)]
    all_to_all x1 -> x5, starting transfers between devices: 6.7 us -> 24.9 us  [swap(): return lax.all_to_all(x, axes, 0, 0, tiled=True)]
    unnamed x26 -> x46, local copies, waits for them, and re-layouts: 9.55 us -> 15.2 us
  transfers between devices with their start and end apart: 2 -> 7, of which waited for: 1 -> 5; matrix products, arithmetic and copies ran while one was open for 0% -> 0% of each run, Pallas kernels for 1% -> 6%
where the time goes in v1:
time: 385 us; the launch traced here: 383 us
  blocking collectives  256 us (66%)
  Pallas kernels  43.1 us (11%)
  waiting for transfers between devices  29.3 us (8%)
  starting transfers between devices  25 us (6%)
  local copies, waits for them, and re-layouts  15.2 us (4%)
  between operations  14.3 us (4%)
    all_to_all x22, blocking collectives, swap(): return lax.all_to_all(x, axes, 0, 0, tiled=True)  256 us
    pallas_call x35, Pallas kernels, call(): pl.pallas_call(body, out_shape=outs, in_specs=[anywhere if i in fetched e...  43.1 us
    all_to_all x5, waiting for transfers between devices, swap(): return lax.all_to_all(x, axes, 0, 0, tiled=True)  28.5 us
    all_to_all x5, starting transfers between devices, swap(): return lax.all_to_all(x, axes, 0, 0, tiled=True)  24.9 us
    unnamed x46, local copies, waits for them, and re-layouts  15.2 us
  transfers between devices with their start and end apart: 7, of which 5 were waited for; matrix products, arithmetic and copies ran while one was open for 0% of the time, Pallas kernels for 6%

profile of v1, /device:TPU:1, one launch (start us, length us, event | category | flops | bytes accessed | tf_op | source)
XLA Modules:
  0.0 383.1 jit_solution(331847043283842029)
XLA Ops:
  13.3 17.9 %all_to_all.135 = bf16[8,32,128]{2,1,0:T(8,128)(2,1)S(1)} all-to-all(bf16[8,32,128]{2,1,0:T(8,128)(2,1)S(1)} %bitcast.81), channel_id=1, replica_groups=mesh['zlo'=4,'x'=4,'y'=8,'zhi'=2,'core'=2] {'zhi','zlo'}, dimensions={0} | all-to-all | bytes 131072 | tf_op jit(solution)/shard_map/all_to_all | solution.py:294
  36.1 22.5 %all_to_all.136.pieces_ref = bf16[64,8,128]{2,1,0:T(8,128)(2,1)S(1)} all-to-all(bf16[64,8,128]{2,1,0:T(8,128)(2,1)S(1)} %bitcast.72), channel_id=1, replica_groups=mesh['zlo'=4,'x'=4,'y'=8,'zhi'=2,'core'=2] {'x','y','core'}, dimensions={0} | all-to-all | bytes 262144 | tf_op jit(solution)/shard_map/all_to_all | solution.py:294
  58.7 10.6 %all_to_all.137.pieces_ref = bf16[16,8,128]{2,1,0:T(8,128)(2,1)S(1)} all-to-all(bf16[16,8,128]{2,1,0:T(8,128)(2,1)S(1)} %shard_map.88), channel_id=1, replica_groups=mesh['zlo'=4,'x'=4,'y'=8,'zhi'=2,'core'=2] {'y','core'}, dimensions={0} | all-to-all | bytes 65536 | tf_op jit(solution)/shard_map/all_to_all | solution.py:294
  71.4 6.7 %all_to_all.138.pieces_ref = bf16[4,32,128]{2,1,0:T(8,128)(2,1)S(1)} all-to-all(bf16[4,32,128]{2,1,0:T(8,128)(2,1)S(1)} %shard_map.89), channel_id=1, replica_groups=mesh['zlo'=4,'x'=4,'y'=8,'zhi'=2,'core'=2] {'x'}, dimensions={0} | all-to-all | bytes 65536 | tf_op jit(solution)/shard_map/all_to_all | solution.py:294
  78.1 13.3 %all_to_all.139 = bf16[16,32,128]{2,1,0:T(8,128)(2,1)S(1)} all-to-all(bf16[16,32,128]{2,1,0:T(8,128)(2,1)S(1)} %shard_map.90), channel_id=1, replica_groups=mesh['zlo'=4,'x'=4,'y'=8,'zhi'=2,'core'=2] {'y','core'}, dimensions={0} | all-to-all | bytes 262144 | tf_op jit(solution)/shard_map/all_to_all | solution.py:294
  91.6 11.4 %all_to_all.140 = bf16[8,32,128]{2,1,0:T(8,128)(2,1)S(1)} all-to-all(bf16[8,32,128]{2,1,0:T(8,128)(2,1)S(1)} %bitcast.79), channel_id=1, replica_groups=mesh['zlo'=4,'x'=4,'y'=8,'zhi'=2,'core'=2] {'zhi','zlo'}, dimensions={0} | all-to-all | bytes 131072 | tf_op jit(solution)/shard_map/all_to_all | solution.py:294
  105.7 10.9 %all_to_all.141 = bf16[8,32,128]{2,1,0:T(8,128)(2,1)S(1)} all-to-all(bf16[8,32,128]{2,1,0:T(8,128)(2,1)S(1)} %bitcast.82), channel_id=1, replica_groups=mesh['zlo'=4,'x'=4,'y'=8,'zhi'=2,'core'=2] {'zhi','zlo'}, dimensions={0} | all-to-all | bytes 131072 | tf_op jit(solution)/shard_map/all_to_all | solution.py:294
  122.9 10.4 %all-to-all-done.7.pieces_ref = bf16[64,8,128]{2,1,0:T(8,128)(2,1)S(1)} async-done(((bf16[64,8,128]{2,1,0:T(8,128)(2,1)}), bf16[64,8,128]{2,1,0:T(8,128)(2,1)S(1)}, u32[]{:S(2)}, u32[]{:S(2)}) %all-to-all-start.7) | async-done | bytes 131104 | tf_op jit(solution)/shard_map/all_to_all | solution.py:294
  133.9 10.6 %all_to_all.142.pieces_ref = bf16[16,8,128]{2,1,0:T(8,128)(2,1)S(1)} all-to-all(bf16[16,8,128]{2,1,0:T(8,128)(2,1)S(1)} %shard_map.94), channel_id=1, replica_groups=mesh['zlo'=4,'x'=4,'y'=8,'zhi'=2,'core'=2] {'y','core'}, dimensions={0} | all-to-all | bytes 65536 | tf_op jit(solution)/shard_map/all_to_all | solution.py:294
  146.5 6.7 %all_to_all.143.pieces_ref = bf16[4,32,128]{2,1,0:T(8,128)(2,1)S(1)} all-to-all(bf16[4,32,128]{2,1,0:T(8,128)(2,1)S(1)} %shard_map.95), channel_id=1, replica_groups=mesh['zlo'=4,'x'=4,'y'=8,'zhi'=2,'core'=2] {'x'}, dimensions={0} | all-to-all | bytes 65536 | tf_op jit(solution)/shard_map/all_to_all | solution.py:294
  168.2 12.0 %all_to_all.144.pieces_ref = bf16[8,64,128]{2,1,0:T(8,128)(2,1)S(1)} all-to-all(bf16[8,64,128]{2,1,0:T(8,128)(2,1)S(1)} %get-tuple-element.28), channel_id=1, replica_groups=mesh['zlo'=4,'x'=4,'y'=8,'zhi'=2,'core'=2] {'zhi','zlo'}, dimensions={0} | all-to-all | bytes 262144 | tf_op jit(solution)/shard_map/all_to_all | solution.py:294
  183.1 14.1 %all_to_all.145.pieces_ref = bf16[64,8,128]{2,1,0:T(8,128)(2,1)S(1)} all-to-all(bf16[64,8,128]{2,1,0:T(8,128)(2,1)S(1)} %bitcast.74), channel_id=1, replica_groups=mesh['zlo'=4,'x'=4,'y'=8,'zhi'=2,'core'=2] {'x','y','core'}, dimensions={0} | all-to-all | bytes 262144 | tf_op jit(solution)/shard_map/all_to_all | solution.py:294
  197.8 10.6 %all_to_all.146.pieces_ref = bf16[16,8,128]{2,1,0:T(8,128)(2,1)S(1)} all-to-all(bf16[16,8,128]{2,1,0:T(8,128)(2,1)S(1)} %shard_map.101), channel_id=1, replica_groups=mesh['zlo'=4,'x'=4,'y'=8,'zhi'=2,'core'=2] {'y','core'}, dimensions={0} | all-to-all | bytes 65536 | tf_op jit(solution)/shard_map/all_to_all | solution.py:294
  208.9 6.7 %all_to_all.147.pieces_ref = bf16[4,32,128]{2,1,0:T(8,128)(2,1)S(1)} all-to-all(bf16[4,32,128]{2,1,0:T(8,128)(2,1)S(1)} %shard_map.102), channel_id=1, replica_groups=mesh['zlo'=4,'x'=4,'y'=8,'zhi'=2,'core'=2] {'x'}, dimensions={0} | all-to-all | bytes 65536 | tf_op jit(solution)/shard_map/all_to_all | solution.py:294
  232.2 12.0 %all_to_all.148.pieces_ref = bf16[8,64,128]{2,1,0:T(8,128)(2,1)S(1)} all-to-all(bf16[8,64,128]{2,1,0:T(8,128)(2,1)S(1)} %get-tuple-element.30), channel_id=1, replica_groups=mesh['zlo'=4,'x'=4,'y'=8,'zhi'=2,'core'=2] {'zhi','zlo'}, dimensions={0} | all-to-all | bytes 262144 | tf_op jit(solution)/shard_map/all_to_all | solution.py:294
  247.2 15.2 %all_to_all.149.pieces_ref = bf16[64,8,128]{2,1,0:T(8,128)(2,1)S(1)} all-to-all(bf16[64,8,128]{2,1,0:T(8,128)(2,1)S(1)} %bitcast.75), channel_id=1, replica_groups=mesh['zlo'=4,'x'=4,'y'=8,'zhi'=2,'core'=2] {'x','y','core'}, dimensions={0} | all-to-all | bytes 262144 | tf_op jit(solution)/shard_map/all_to_all | solution.py:294
  263.3 10.6 %all_to_all.150.pieces_ref = bf16[16,8,128]{2,1,0:T(8,128)(2,1)S(1)} all-to-all(bf16[16,8,128]{2,1,0:T(8,128)(2,1)S(1)} %shard_map.108), channel_id=1, replica_groups=mesh['zlo'=4,'x'=4,'y'=8,'zhi'=2,'core'=2] {'y','core'}, dimensions={0} | all-to-all | bytes 65536 | tf_op jit(solution)/shard_map/all_to_all | solution.py:294
  274.4 6.7 %all_to_all.151.pieces_ref = bf16[4,32,128]{2,1,0:T(8,128)(2,1)S(1)} all-to-all(bf16[4,32,128]{2,1,0:T(8,128)(2,1)S(1)} %shard_map.109), channel_id=1, replica_groups=mesh['zlo'=4,'x'=4,'y'=8,'zhi'=2,'core'=2] {'x'}, dimensions={0} | all-to-all | bytes 65536 | tf_op jit(solution)/shard_map/all_to_all | solution.py:294
  297.7 12.0 %all_to_all.152.pieces_ref = bf16[8,64,128]{2,1,0:T(8,128)(2,1)S(1)} all-to-all(bf16[8,64,128]{2,1,0:T(8,128)(2,1)S(1)} %get-tuple-element.32), channel_id=1, replica_groups=mesh['zlo'=4,'x'=4,'y'=8,'zhi'=2,'core'=2] {'zhi','zlo'}, dimensions={0} | all-to-all | bytes 262144 | tf_op jit(solution)/shard_map/all_to_all | solution.py:294
  312.7 15.1 %all_to_all.153.pieces_ref = bf16[64,8,128]{2,1,0:T(8,128)(2,1)S(1)} all-to-all(bf16[64,8,128]{2,1,0:T(8,128)(2,1)S(1)} %bitcast.73), channel_id=1, replica_groups=mesh['zlo'=4,'x'=4,'y'=8,'zhi'=2,'core'=2] {'x','y','core'}, dimensions={0} | all-to-all | bytes 262144 | tf_op jit(solution)/shard_map/all_to_all | solution.py:294
  328.8 10.6 %all_to_all.154.pieces_ref = bf16[16,8,128]{2,1,0:T(8,128)(2,1)S(1)} all-to-all(bf16[16,8,128]{2,1,0:T(8,128)(2,1)S(1)} %shard_map.115), channel_id=1, replica_groups=mesh['zlo'=4,'x'=4,'y'=8,'zhi'=2,'core'=2] {'y','core'}, dimensions={0} | all-to-all | bytes 65536 | tf_op jit(solution)/shard_map/all_to_all | solution.py:294
  339.8 6.7 %all_to_all.155.pieces_ref = bf16[4,32,128]{2,1,0:T(8,128)(2,1)S(1)} all-to-all(bf16[4,32,128]{2,1,0:T(8,128)(2,1)S(1)} %shard_map.116), channel_id=1, replica_groups=mesh['zlo'=4,'x'=4,'y'=8,'zhi'=2,'core'=2] {'x'}, dimensions={0} | all-to-all | bytes 65536 | tf_op jit(solution)/shard_map/all_to_all | solution.py:294
  346.5 13.3 %all_to_all.156 = bf16[16,32,128]{2,1,0:T(8,128)(2,1)S(1)} all-to-all(bf16[16,32,128]{2,1,0:T(8,128)(2,1)S(1)} %get-tuple-element.34), channel_id=1, replica_groups=mesh['zlo'=4,'x'=4,'y'=8,'zhi'=2,'core'=2] {'y','core'}, dimensions={0} | all-to-all | bytes 262144 | tf_op jit(solution)/shard_map/all_to_all | solution.py:294
  366.8 5.9 %all-to-all-done.26.pieces_ref = bf16[8,48,128]{2,1,0:T(8,128)(2,1)S(1)} async-done(((bf16[8,48,128]{2,1,0:T(8,128)(2,1)}), bf16[8,48,128]{2,1,0:T(8,128)(2,1)S(1)}, u32[]{:S(2)}, u32[]{:S(2)}) %all-to-all-start.26) | async-done | bytes 98336 | tf_op jit(solution)/shard_map/all_to_all | solution.py:294
  (96 shorter events, 96.4 us)
Async XLA Ops:
  7.2 62.2 %all-gather.5.cloned.1.call-start = ((), (), s32[]{:S(2)}) async-start(), calls=%async_computation.27 | async-start | bytes 2359296 | tf_op jit(solution)/shard_map/all_gather | solution.py:306
  7.9 172.3 %all-gather.7.cloned.1.call-start = ((), (), s32[]{:S(2)}) async-start(), calls=%async_computation.28 | async-start | bytes 4718592 | tf_op jit(solution)/shard_map/all_gather | solution.py:334
  8.6 23.2 %copy-start = (bf16[1,4,512,512]{3,2,1,0:T(8,128)(2,1)S(1)}, bf16[1,4,512,512]{3,2,1,0:T(8,128)(2,1)}, u32[]{:S(2)}) copy-start(bf16[1,4,512,512]{3,2,1,0:T(8,128)(2,1)} %param.7) | copy-start | bytes 6291460
  8.6 23.2 %copy-start.1 = (bf16[1,512,2048]{2,1,0:T(8,128)(2,1)S(1)}, bf16[1,512,2048]{2,1,0:T(8,128)(2,1)}, u32[]{:S(2)}) copy-start(bf16[1,512,2048]{2,1,0:T(8,128)(2,1)} %param.8) | copy-start | bytes 6291460
  8.6 23.2 %copy-start.19 = (f32[1,2048]{1,0:T(1,128)S(1)}, f32[1,2048]{1,0:T(1,128)}, u32[]{:S(2)}) copy-start(f32[1,2048]{1,0:T(1,128)} %scale_ref.15) | copy-start | bytes 24580
  36.1 66.9 %copy-start.13 = (bf16[1,48,2048]{2,1,0:T(8,128)(2,1)S(1)}, bf16[1,48,2048]{2,1,0:T(8,128)(2,1)}, u32[]{:S(2)}) copy-start(bf16[1,48,2048]{2,1,0:T(8,128)(2,1)} %param.10) | copy-start | bytes 589828
  69.3 33.7 %copy-start.2 = (bf16[1,512,2048]{2,1,0:T(8,128)(2,1)S(1)}, bf16[1,512,2048]{2,1,0:T(8,128)(2,1)}, u32[]{:S(2)}) copy-start(bf16[1,512,2048]{2,1,0:T(8,128)(2,1)} %param.8) | copy-start | bytes 6291460
  69.3 1.7 copy-start.8
  103.0 30.2 %copy-start.20 = (f32[8192]{0:T(1024)S(1)}, f32[8192]{0:T(1024)}, u32[]{:S(2)}) copy-start(f32[8192]{0:T(1024)} %param.12) | copy-start | bytes 98308
  105.7 56.8 %copy-start.17 = (bf16[48,2048]{1,0:T(8,128)(2,1)}, bf16[48,2048]{1,0:T(8,128)(2,1)S(1)}, u32[]{:S(2)}) copy-start(bf16[48,2048]{1,0:T(8,128)(2,1)S(1)} %get-tuple-element.27.corrected_ref) | copy-start | bytes 589828
  117.4 15.8 %all-to-all-start.7 = ((bf16[64,8,128]{2,1,0:T(8,128)(2,1)}), bf16[64,8,128]{2,1,0:T(8,128)(2,1)S(1)}, u32[]{:S(2)}, u32[]{:S(2)}) async-start(bf16[64,8,128]{2,1,0:T(8,128)(2,1)} %bitcast.71), calls=%async_computation.7 | async-start | bytes 262144 | tf_op jit(solution)/shard_map/all_to_all | solution.py:294
  144.5 1.6 copy-start.9
  153.8 14.2 %all-to-all-start.10 = ((bf16[16,32,128]{2,1,0:T(8,128)(2,1)}), bf16[16,32,128]{2,1,0:T(8,128)(2,1)S(1)}, u32[]{:S(2)}, u32[]{:S(2)}) async-start(bf16[16,32,128]{2,1,0:T(8,128)(2,1)} %shard_map.96), calls=%async_computation.10 | async-start | bytes 262144 | tf_op jit(solution)/shard_map/all_to_all | solution.py:294
  158.8 1.6 copy-start.3
  180.2 28.3 %copy-start.10 = (bf16[4096,256]{1,0:T(8,128)(2,1)S(1)}, bf16[4096,256]{1,0:T(8,128)(2,1)}, u32[]{:S(2)}) copy-start(bf16[4096,256]{1,0:T(8,128)(2,1)} %all-gather.5.cloned.1.call-done) | copy-start | bytes 6291460
  216.2 14.9 %all-to-all-start.15 = ((bf16[16,32,128]{2,1,0:T(8,128)(2,1)}), bf16[16,32,128]{2,1,0:T(8,128)(2,1)}, u32[]{:S(2)}, u32[]{:S(2)}) async-start(bf16[16,32,128]{2,1,0:T(8,128)(2,1)} %shard_map.103), calls=%async_computation.15 | async-start | bytes 262144 | tf_op jit(solution)/shard_map/all_to_all | solution.py:294
  221.8 1.6 copy-start.4
  244.2 3.0 copy-start.15
  244.2 29.8 %copy-start.11 = (bf16[4096,256]{1,0:T(8,128)(2,1)S(1)}, bf16[4096,256]{1,0:T(8,128)(2,1)}, u32[]{:S(2)}) copy-start(bf16[4096,256]{1,0:T(8,128)(2,1)} %all-gather.5.cloned.1.call-done) | copy-start | bytes 6291460
  281.7 14.9 %all-to-all-start.20 = ((bf16[16,32,128]{2,1,0:T(8,128)(2,1)}), bf16[16,32,128]{2,1,0:T(8,128)(2,1)}, u32[]{:S(2)}, u32[]{:S(2)}) async-start(bf16[16,32,128]{2,1,0:T(8,128)(2,1)} %shard_map.110), calls=%async_computation.20 | async-start | bytes 262144 | tf_op jit(solution)/shard_map/all_to_all | solution.py:294
  309.7 29.7 %copy-start.12 = (bf16[4096,256]{1,0:T(8,128)(2,1)S(1)}, bf16[4096,256]{1,0:T(8,128)(2,1)}, u32[]{:S(2)}) copy-start(bf16[4096,256]{1,0:T(8,128)(2,1)} %all-gather.5.cloned.1.call-done) | copy-start | bytes 6291460
  360.6 12.1 %all-to-all-start.26 = ((bf16[8,48,128]{2,1,0:T(8,128)(2,1)}), bf16[8,48,128]{2,1,0:T(8,128)(2,1)S(1)}, u32[]{:S(2)}, u32[]{:S(2)}) async-start(bf16[8,48,128]{2,1,0:T(8,128)(2,1)} %shard_map.118), calls=%async_computation.26 | async-start | bytes 196608 | tf_op jit(solution)/shard_map/all_to_all | solution.py:294
  364.0 1.6 copy-start.6
  372.8 1.6 copy-start.7
  (6 other events, 5.5 us)
Sparse Core Ops, SparseCore 0:
  10.1 45.3 all-gather.4
  57.5 63.1 all-gather.6

commit v2 on v1

--- a/solution.py
+++ b/solution.py
@@ -59,18 +59,17 @@
     ).astype(BF16)
 
 
-def touched_pieces(corrected, tile_ref, coupling_ref, pack):
-    solved = by_tiles(tile_ref, corrected)
+def touched_pieces(solved, coupling_ref, pack):
     touched = dot_t(solved, coupling_ref[...]).astype(BF16)
     rows = jnp.concatenate([touched[:, s * PANEL : (s + 1) * PANEL] for s in range(PB)], axis=0)
     return dot(pack, rows)
 
 
-def solve_leaf(rows, corrected_ref, tile_ref, coupling_ref):
-    columns = corrected_ref.shape[0]
+def solve_leaf(rows, corrected, tile_ref, coupling_ref):
+    columns = corrected.shape[0]
     picked = jnp.concatenate([rows[s * columns : (s + 1) * columns] for s in range(PB)], axis=1)
     pushed = dot(picked, coupling_ref[...])
-    reduced = (corrected_ref[...].astype(F32) - pushed).astype(BF16)
+    reduced = (corrected.astype(F32) - pushed).astype(BF16)
     return by_tiles(tile_ref, reduced)
 
 
@@ -97,7 +96,7 @@
     unpack_ref[...] = unpacker(PB)
     for fetch in fetches:
         fetch.wait()
-    pieces = touched_pieces(rhs_ref[...], tile_ref, coupling_ref, pack)
+    pieces = touched_pieces(by_tiles(tile_ref, rhs_ref[...]), coupling_ref, pack)
     row = iota(pieces.shape, 0)
     for s in range(PB):
         here = row % (PB * ROWS) == s * ROWS + PER_SET
@@ -167,96 +166,146 @@
     own_ref[...] = total
 
 
-def last_pick_kernel(select_ref, pieces_ref, own_ref, out_ref):
-    picked = dot(select_ref[...], pieces_ref[...]).astype(BF16)
-    size = picked.shape[0] // SETS
+def last_pick_kernel(select_ref, pieces_ref, own_ref, *refs):
+    out_ref, size = refs[-1], PB * ROWS
+    picked = [ref[...] for ref in refs[:-1]]
+    picked.append(dot(select_ref[...], pieces_ref[...]).astype(BF16))
     for zi in range(SETS):
         half = (zi // 4) * 2 * ROWS
-        out_ref[zi, :size] = picked[zi * size : (zi + 1) * size]
-        out_ref[zi, size:] = own_ref[half : half + 2 * ROWS]
+        for k, rows in enumerate(picked):
+            out_ref[zi, k * size : (k + 1) * size] = rows[zi * size : (zi + 1) * size]
+        out_ref[zi, len(picked) * size :] = own_ref[half : half + 2 * ROWS]
 
 
 def correct(rhs_ref, scale_ref, leaf):
     return (rhs_ref[...].astype(F32) - scale_ref[...] * leaf.astype(F32)).astype(BF16)
 
 
-def ahead_pieces(corrected, rhs_ref, scale_ref, tile_ref, coupling_ref, pack):
-    leaf = by_tiles(tile_ref, corrected)
-    return touched_pieces(correct(rhs_ref, scale_ref, leaf), tile_ref, coupling_ref, pack)
-
-
-def response_kernel(after_ref, scale_ref, tile_ref, coupling_ref, out_ref):
-    leaf = by_tiles(tile_ref, coupling_ref[...])
-    moved = (scale_ref[...] * leaf.astype(F32)).astype(BF16)
-    solved = by_tiles(tile_ref, moved)
-    out_ref[...] = dot_t(solved, coupling_ref[...]).astype(BF16)
-
-
-def middle_kernel(
-    pieces_ref, unpack_ref, pack_ref, corrected_ref, rhs_ref, scale_ref, tile_ref, coupling_ref,
-    out_ref, next_ref,
+def in_chunks(body, rows, chunk=256):
+    def step(i, carry):
+        body(pl.ds(pl.multiple_of(i * chunk, chunk), chunk))
+        return carry
+
+    lax.fori_loop(0, rows // chunk, step, 0)
+
+
+def first_response_kernel(after_ref, scale_ref, tile_ref, coupling_ref, out_ref, solved_ref):
+    def some(rows):
+        leaf = by_tiles(tile_ref, coupling_ref[rows, :])
+        solved = by_tiles(tile_ref, (scale_ref[...] * leaf.astype(F32)).astype(BF16))
+        solved_ref[rows, :] = solved
+        out_ref[rows, :] = dot_t(solved, coupling_ref[...]).astype(BF16)
+
+    in_chunks(some, out_ref.shape[0])
+
+
+def response_kernel(after_ref, earlier_ref, scale_ref, tile_ref, coupling_ref, out_ref, solved_ref):
+    def some(rows):
+        moved = (-scale_ref[...] * earlier_ref[rows, :].astype(F32)).astype(BF16)
+        solved = by_tiles(tile_ref, moved)
+        solved_ref[rows, :] = solved
+        out_ref[rows, :] = dot_t(solved, coupling_ref[...]).astype(BF16)
+
+    in_chunks(some, out_ref.shape[0])
+
+
+def ahead_kernel(
+    pieces_ref, unpack_ref, pack_ref, rhs_ref, scale_ref, tile_ref, coupling_ref,
+    out_ref, next_ref, state_ref,
 ):
+    size = PB * ROWS
     rows = dot(unpack_ref[...], pieces_ref[...]).astype(BF16)
-    leaf = solve_leaf(rows, corrected_ref, tile_ref, coupling_ref)
+    leaf = solve_leaf(rows, rhs_ref[...], tile_ref, coupling_ref)
     corrected = correct(rhs_ref, scale_ref, leaf)
     next_ref[...] = corrected
-    out_ref[...] = touched_pieces(corrected, tile_ref, coupling_ref, pack_ref[...]).astype(BF16)
-
-
-def ahead_kernel(
-    pack_ref, corrected_ref, rhs_ref, scale_ref, tile_ref, coupling_ref, out_ref
-):
-    out_ref[...] = ahead_pieces(
-        corrected_ref[...], rhs_ref, scale_ref, tile_ref, coupling_ref, pack_ref[...]
-    ).astype(BF16)
-
-
-def home_kernel(
-    pieces_ref, unpack_ref, corrected_ref, rhs_ref, scale_ref, tile_ref, coupling_ref, next_ref
-):
+    state_ref[...] = corrected
+
+    def solve(k, carry):
+        solved = by_tiles(tile_ref, state_ref[...])
+        state_ref[...] = correct(rhs_ref, scale_ref, solved)
+        pieces = touched_pieces(solved, coupling_ref, pack_ref[...]).astype(BF16)
+        rows = pl.ds(pl.multiple_of(k * size, size), size)
+        for zi in range(SETS):
+            out_ref[zi, rows, :] = pieces[zi * size : (zi + 1) * size]
+        return carry
+
+    lax.fori_loop(0, SOLVES - 1, solve, 0)
+
+
+def ahead_rows(ahead_ref, k):
     size = PB * ROWS
-    pieces = jnp.concatenate([pieces_ref[zi, :size] for zi in range(SETS)], axis=0)
-    rows = dot(unpack_ref[...], pieces).astype(BF16)
-    leaf = solve_leaf(rows, corrected_ref, tile_ref, coupling_ref)
-    next_ref[...] = correct(rhs_ref, scale_ref, leaf)
-
-
-def both_pick_kernel(select_ref, pieces_ref, ahead_ref, out_ref, picked_ref):
-    picked = dot(select_ref[...], pieces_ref[...]).astype(BF16)
-    picked_ref[...] = picked
-    size = PB * ROWS
-    for zi in range(SETS):
-        out_ref[zi, :size] = picked[zi * size : (zi + 1) * size]
-        out_ref[zi, size:] = ahead_ref[zi * size : (zi + 1) * size]
-
-
-def respond_kernel(pieces_ref, picked_ref, spread_ref, response_hbm, out_ref, response_ref, sems):
-    size, rows = PB * ROWS, []
+    return jnp.concatenate(
+        [ahead_ref[zi, (k - 1) * size : k * size] for zi in range(SETS)], axis=0
+    )
+
+
+def ahead_spread_kernel(spread_ref, ahead_ref, out_ref):
+    out_ref[...] = dot(spread_ref[...], ahead_rows(ahead_ref, 1)).astype(BF16)
+
+
+def fetch_all(response_hbm, response_ref, sems):
     fetches = [
         pltpu.make_async_copy(response_hbm.at[zi], response_ref.at[zi], sems.at[zi])
         for zi in range(SETS)
     ]
     for fetch in fetches:
         fetch.start()
+    return fetches
+
+
+def responses(fetches, picked_ref, response_ref):
+    rows = []
     for zi in range(SETS):
-        places = [slice(s * ROWS, (s + 1) * ROWS) for s in range(PB)]
-        picked = jnp.concatenate([picked_ref[zi * size + p.start : zi * size + p.stop] for p in places], axis=1)
+        starts = [(zi * PB + s) * ROWS for s in range(PB)]
+        picked = jnp.concatenate([picked_ref[r : r + ROWS] for r in starts], axis=1)
         fetches[zi].wait()
         added = dot(picked, response_ref[zi])
-        added = jnp.concatenate([added[:, s * PANEL : (s + 1) * PANEL] for s in range(PB)], axis=0)
-        rows.append((pieces_ref[zi, size:].astype(F32) + added).astype(BF16))
-    out_ref[...] = dot(spread_ref[...], jnp.concatenate(rows, axis=0)).astype(BF16)
+        rows += [added[:, s * PANEL : (s + 1) * PANEL] for s in range(PB)]
+    return jnp.concatenate(rows, axis=0)
+
+
+def respond_kernel(base_ref, picked_ref, spread_ref, response_hbm, out_ref, response_ref, sems):
+    fetches = fetch_all(response_hbm, response_ref, sems)
+    base = ahead_rows(base_ref, 2) if base_ref.ndim == 3 else base_ref[...]
+    touched = base.astype(F32) + responses(fetches, picked_ref, response_ref)
+    out_ref[...] = dot(spread_ref[...], touched.astype(BF16)).astype(BF16)
+
+
+def third_base_kernel(ahead_ref, picked_ref, response_hbm, out_ref, response_ref, sems):
+    fetches = fetch_all(response_hbm, response_ref, sems)
+    added = responses(fetches, picked_ref, response_ref)
+    out_ref[...] = ahead_rows(ahead_ref, 3).astype(F32) + added
+
+
+def fourth_base_kernel(
+    ahead_ref, near_ref, far_ref, near_hbm, far_hbm, out_ref,
+    near_response_ref, far_response_ref, near_sems, far_sems,
+):
+    near = fetch_all(near_hbm, near_response_ref, near_sems)
+    far = fetch_all(far_hbm, far_response_ref, far_sems)
+    added = responses(near, near_ref, near_response_ref)
+    added = added + responses(far, far_ref, far_response_ref)
+    out_ref[...] = ahead_rows(ahead_ref, 4).astype(F32) + added
 
 
 def last_kernel(
-    pieces_ref, unpack_ref, corrected_ref, tile_ref, coupling_ref, leaf_ref, link_ref
+    pieces_ref, unpack_ref, corrected_ref, rhs_ref, scale_ref, tile_ref, coupling_ref,
+    leaf_ref, link_ref, state_ref,
 ):
-    columns = corrected_ref.shape[0]
-    size = PB * ROWS
-    pieces = jnp.concatenate([pieces_ref[zi, :size] for zi in range(SETS)], axis=0)
-    rows = dot(unpack_ref[...], pieces).astype(BF16)
-    leaf_ref[...] = solve_leaf(rows, corrected_ref, tile_ref, coupling_ref)
-    link = jnp.concatenate([pieces_ref[zi, size:] for zi in range(SETS)], axis=0)
+    columns, size = corrected_ref.shape[0], PB * ROWS
+    state_ref[...] = corrected_ref[...]
+
+    def solve(k, carry):
+        at = pl.ds(pl.multiple_of(k * size, size), size)
+        pieces = jnp.concatenate([pieces_ref[zi, at, :] for zi in range(SETS)], axis=0)
+        rows = dot(unpack_ref[...], pieces).astype(BF16)
+        leaf = solve_leaf(rows, state_ref[...], tile_ref, coupling_ref)
+        leaf_ref[...] = leaf
+        state_ref[...] = correct(rhs_ref, scale_ref, leaf)
+        return carry
+
+    lax.fori_loop(0, SOLVES - 1, solve, 0)
+    link = jnp.concatenate([pieces_ref[zi, (SOLVES - 1) * size :] for zi in range(SETS)], axis=0)
     link = dot(unpacker(2), link).astype(BF16)
     link_ref[...] = jnp.concatenate([link[:columns], link[columns:]], axis=1)
 
@@ -264,8 +313,8 @@
 INTERPRET = False
 
 
-def call(body, shapes, *operands, fetched=()):
-    outs = [jax.ShapeDtypeStruct(s, BF16) for s in shapes]
+def call(body, shapes, *operands, fetched=(), queues=1, state=(), dtype=BF16):
+    outs = [jax.ShapeDtypeStruct(s, dtype) for s in shapes]
     vmem, smem, anywhere = (
         pl.BlockSpec(memory_space=s) for s in (pltpu.VMEM, pltpu.SMEM, pltpu.HBM)
     )
@@ -273,9 +322,10 @@
         pltpu.with_memory_space_constraint(x, pltpu.HBM) if i in fetched and not INTERPRET else x
         for i, x in enumerate(operands)
     ]
-    scratch = [pltpu.VMEM(operands[i].shape, BF16) for i in fetched]
+    scratch = [pltpu.VMEM(s, BF16) for s in state]
+    scratch += [pltpu.VMEM(operands[i].shape, BF16) for i in fetched]
     if fetched:
-        scratch.append(pltpu.SemaphoreType.DMA((SETS,)))
+        scratch += [pltpu.SemaphoreType.DMA((SETS,))] * queues
     return pl.pallas_call(
         body,
         out_shape=outs,
@@ -314,30 +364,36 @@
     flat = (members * ROWS, PANEL)
     mixer = (PB * columns, SETS * PB * ROWS)
     parts = (4 * ROWS, PANEL)
-    corrected = own_rhs
     pieces, pack, unpack = call(
         first_kernel, [home, mixer[::-1], mixer], link_panels, own_rhs, tile_inv, coupling,
         fetched=(1, 2, 3),
     )
-    for solve_index in range(SOLVES):
-        last = solve_index == SOLVES - 1
-        if solve_index < 2:
-            pieces = swap(pieces.reshape(SETS, PB * ROWS, PANEL), Z).reshape(home)
-        if solve_index == 0:
+    sent = (SETS, PB * ROWS, PANEL)
+    blocks = (leaf_scale, tile_inv, coupling)
+    answers, picks = [], []
+    for k in range(SOLVES):
+        last = k == SOLVES - 1
+        if k == 0:
             pieces, spread, pick = call(
-                first_spread_kernel, [flat, (flat[0], home[0]), (home[0], flat[0])], pieces
+                first_spread_kernel, [flat, (flat[0], home[0]), (home[0], flat[0])],
+                swap(pieces.reshape(sent), Z).reshape(home),
             )
-            response, = call(
-                response_kernel, [(PB * PANEL,) * 2],
-                pieces, leaf_scale, tile_inv, coupling,
+        elif k == 1:
+            pieces, = call(ahead_spread_kernel, [flat], spread, ahead)
+        else:
+            base = ahead if k == 2 else base
+            pieces, = call(
+                respond_kernel, [flat], base, picks[-1], spread, answers[0], fetched=(3,)
             )
-            response = lax.all_gather(response, Z)
-        elif solve_index == 1:
-            pieces, = call(select_kernel, [flat], spread, pieces)
-        else:
-            pieces, = call(respond_kernel, [flat], both, picked, spread, response, fetched=(3,))
+        if k < 3:
+            answer = [(PB * PANEL,) * 2, (PB * PANEL, own_rhs.shape[1])]
+            if k == 0:
+                answer, solved = call(first_response_kernel, answer, pieces, *blocks)
+            else:
+                answer, solved = call(response_kernel, answer, pieces, solved, *blocks)
+            answers.append(lax.all_gather(answer, Z))
         pieces = swap(pieces.reshape(members, ROWS, PANEL), GROUP)
-        if solve_index == 0:
+        if k == 0:
             pieces, = call(first_rhs_kernel, [(line, ROWS, PANEL)], pieces)
         else:
             pieces, = call(rhs_kernel, [(line, ROWS, PANEL)], where, pieces, step, scales)
@@ -349,33 +405,36 @@
         else:
             pieces, = call(total_kernel, [(line,) + parts], pieces)
         pieces = swap(pieces, LINE)
+        if k == 2:
+            base, = call(
+                third_base_kernel, [home], ahead, picks[0], answers[1],
+                fetched=(2,), dtype=F32,
+            )
+        elif k == 3:
+            base, = call(
+                fourth_base_kernel, [home],
+                ahead, picks[1], picks[0], answers[1], answers[2],
+                fetched=(3, 4), queues=2, dtype=F32,
+            )
         step, pieces = pieces.reshape(members, ROWS, PANEL), pieces.reshape(flat)
         if last:
-            wide = (SETS, (PB + 2) * ROWS, PANEL)
-            pieces, = call(last_pick_kernel, [wide], pick, pieces, own)
+            wide = (SETS, ((SOLVES - 1) * PB + 2) * ROWS, PANEL)
+            pieces, = call(last_pick_kernel, [wide], pick, pieces, own, *picks)
             leaf, link = call(
                 last_kernel, [own_rhs.shape, (columns, 2 * PANEL)],
-                swap(pieces, Z), unpack, corrected, tile_inv, coupling,
-            )
-        elif solve_index == 0:
-            pieces, = call(select_kernel, [home], pick, pieces)
-            pieces = swap(pieces.reshape(SETS, PB * ROWS, PANEL), Z).reshape(home)
-            pieces, corrected = call(
-                middle_kernel, [home, own_rhs.shape],
-                pieces, unpack, pack, corrected, own_rhs, leaf_scale, tile_inv, coupling,
+                swap(pieces, Z), unpack, corrected, own_rhs, *blocks, state=(own_rhs.shape,),
             )
         else:
-            both = (SETS, 2 * PB * ROWS, PANEL)
-            ahead, = call(
-                ahead_kernel, [home],
-                pack, corrected, own_rhs, leaf_scale, tile_inv, coupling,
-            )
-            both, picked = call(both_pick_kernel, [both, home], pick, pieces, ahead)
-            both = swap(both, Z)
-            corrected, = call(
-                home_kernel, [own_rhs.shape],
-                both, unpack, corrected, own_rhs, leaf_scale, tile_inv, coupling,
-            )
+            picked, = call(select_kernel, [home], pick, pieces)
+            if k == 0:
+                ahead, corrected = call(
+                    ahead_kernel, [(SETS, (SOLVES - 1) * PB * ROWS, PANEL), own_rhs.shape],
+                    swap(picked.reshape(sent), Z).reshape(home),
+                    unpack, pack, own_rhs, *blocks, state=(own_rhs.shape,),
+                )
+                ahead = swap(ahead, Z)
+            else:
+                picks.append(picked)
     return leaf[None], link
 
 

time: 385 us -> 374 us (0.971)
  blocking collectives: 256 us -> 277 us
  waiting for transfers between devices: 29.3 us -> 11.1 us
  starting transfers between devices: 25 us -> 7.31 us
  Pallas kernels: 43.1 us -> 51.7 us
    all_to_all x22 -> x23, blocking collectives: 256 us -> 277 us  [swap(): return lax.all_to_all(x, axes, 0, 0, tiled=True)]
    all_to_all x5 -> x1, waiting for transfers between devices: 28.5 us -> 10.3 us  [swap(): return lax.all_to_all(x, axes, 0, 0, tiled=True)]
    all_to_all x5 -> x1, starting transfers between devices: 24.9 us -> 7.15 us  [swap(): return lax.all_to_all(x, axes, 0, 0, tiled=True)]
    pallas_call x35 -> x33, Pallas kernels: 43.1 us -> 51.7 us  [call(): pl.pallas_call(body, out_shape=outs, in_specs=[anywhere if i in fetched e...]
    unnamed x46 -> x50, local copies, waits for them, and re-layouts: 15.2 us -> 12.2 us
  transfers between devices with their start and end apart: 7 -> 5, of which waited for: 5 -> 1; matrix products, arithmetic and copies ran while one was open for 0% -> 0% of each run, Pallas kernels for 6% -> 10%
where the time goes in v2:
time: 374 us; the launch traced here: 373 us
  blocking collectives  277 us (74%)
  Pallas kernels  51.7 us (14%)
  between operations  14.1 us (4%)
  local copies, waits for them, and re-layouts  12.2 us (3%)
  waiting for transfers between devices  11.1 us (3%)
  starting transfers between devices  7.31 us (2%)
    all_to_all x23, blocking collectives, swap(): return lax.all_to_all(x, axes, 0, 0, tiled=True)  277 us
    pallas_call x33, Pallas kernels, call(): pl.pallas_call(body, out_shape=outs, in_specs=[anywhere if i in fetched e...  51.7 us
    unnamed x50, local copies, waits for them, and re-layouts  12.2 us
    all_to_all x1, waiting for transfers between devices, swap(): return lax.all_to_all(x, axes, 0, 0, tiled=True)  10.3 us
  transfers between devices with their start and end apart: 5, of which 1 were waited for; matrix products, arithmetic and copies ran while one was open for 0% of the time, Pallas kernels for 10%

profile of v2, /device:TPU:1, one launch (start us, length us, event | category | flops | bytes accessed | tf_op | source)
XLA Modules:
  0.0 373.1 jit_solution(15471393700030181990)
XLA Ops:
  13.3 17.9 %all_to_all.120 = bf16[8,32,128]{2,1,0:T(8,128)(2,1)S(1)} all-to-all(bf16[8,32,128]{2,1,0:T(8,128)(2,1)S(1)} %bitcast.69), channel_id=1, replica_groups=mesh['zlo'=4,'x'=4,'y'=8,'zhi'=2,'core'=2] {'zhi','zlo'}, dimensions={0} | all-to-all | bytes 131072 | tf_op jit(solution)/shard_map/all_to_all | solution.py:344
  37.8 22.5 %all_to_all.121.pieces_ref = bf16[64,8,128]{2,1,0:T(8,128)(2,1)S(1)} all-to-all(bf16[64,8,128]{2,1,0:T(8,128)(2,1)S(1)} %bitcast.62), channel_id=1, replica_groups=mesh['zlo'=4,'x'=4,'y'=8,'zhi'=2,'core'=2] {'x','y','core'}, dimensions={0} | all-to-all | bytes 262144 | tf_op jit(solution)/shard_map/all_to_all | solution.py:344
  60.3 10.6 %all_to_all.122.pieces_ref = bf16[16,8,128]{2,1,0:T(8,128)(2,1)S(1)} all-to-all(bf16[16,8,128]{2,1,0:T(8,128)(2,1)S(1)} %shard_map.88), channel_id=1, replica_groups=mesh['zlo'=4,'x'=4,'y'=8,'zhi'=2,'core'=2] {'y','core'}, dimensions={0} | all-to-all | bytes 65536 | tf_op jit(solution)/shard_map/all_to_all | solution.py:344
  73.1 6.7 %all_to_all.123.pieces_ref = bf16[4,32,128]{2,1,0:T(8,128)(2,1)S(1)} all-to-all(bf16[4,32,128]{2,1,0:T(8,128)(2,1)S(1)} %shard_map.89), channel_id=1, replica_groups=mesh['zlo'=4,'x'=4,'y'=8,'zhi'=2,'core'=2] {'x'}, dimensions={0} | all-to-all | bytes 65536 | tf_op jit(solution)/shard_map/all_to_all | solution.py:344
  79.8 13.2 %all_to_all.124 = bf16[16,32,128]{2,1,0:T(8,128)(2,1)S(1)} all-to-all(bf16[16,32,128]{2,1,0:T(8,128)(2,1)S(1)} %shard_map.90), channel_id=1, replica_groups=mesh['zlo'=4,'x'=4,'y'=8,'zhi'=2,'core'=2] {'y','core'}, dimensions={0} | all-to-all | bytes 262144 | tf_op jit(solution)/shard_map/all_to_all | solution.py:344
  93.3 11.4 %all_to_all.125 = bf16[8,32,128]{2,1,0:T(8,128)(2,1)S(1)} all-to-all(bf16[8,32,128]{2,1,0:T(8,128)(2,1)S(1)} %bitcast.67), channel_id=1, replica_groups=mesh['zlo'=4,'x'=4,'y'=8,'zhi'=2,'core'=2] {'zhi','zlo'}, dimensions={0} | all-to-all | bytes 131072 | tf_op jit(solution)/shard_map/all_to_all | solution.py:344
  105.6 7.4 %shard_map.92 = (bf16[8,128,128]{2,1,0:T(8,128)(2,1)S(1)}, bf16[48,2048]{1,0:T(8,128)(2,1)S(1)}) custom-call(bf16[256,128]{1,0:T(8,128)(2,1)S(1)} %bitcast.66, bf16[192,256]{1,0:T(8,128)(2,1)S(1)} %get-tuple-element.22.unpack_ref, bf16[256,192]{1,0:T(8,128)(2,1)S(1)} %copy-done.23, bf16[48,2048]{1,0:T(8,128)(2,1)S(1)} %bitcast.47, f32[1,2048]{1,0:T(1,128)S(1)} %copy-done.19, ...), custom_call_target="tpu_custom_call" | custom-call | tf_op jit(solution)/shard_map/pallas_call | solution.py:329
  113.0 14.7 %all_to_all.126.ahead_ref.base_ref = bf16[8,128,128]{2,1,0:T(8,128)(2,1)S(1)} all-to-all(bf16[8,128,128]{2,1,0:T(8,128)(2,1)S(1)} %get-tuple-element.24), channel_id=1, replica_groups=mesh['zlo'=4,'x'=4,'y'=8,'zhi'=2,'core'=2] {'zhi','zlo'}, dimensions={0} | all-to-all | bytes 524288 | tf_op jit(solution)/shard_map/all_to_all | solution.py:344
  134.2 7.1 %all-to-all-start.7 = ((bf16[64,8,128]{2,1,0:T(8,128)(2,1)}), bf16[64,8,128]{2,1,0:T(8,128)(2,1)S(1)}, u32[]{:S(2)}, u32[]{:S(2)}) async-start(bf16[64,8,128]{2,1,0:T(8,128)(2,1)} %bitcast.12), calls=%async_computation.7 | async-start | bytes 262144 | tf_op jit(solution)/shard_map/all_to_all | solution.py:344
  141.5 10.3 %all-to-all-done.7.pieces_ref = bf16[64,8,128]{2,1,0:T(8,128)(2,1)S(1)} async-done(((bf16[64,8,128]{2,1,0:T(8,128)(2,1)}), bf16[64,8,128]{2,1,0:T(8,128)(2,1)S(1)}, u32[]{:S(2)}, u32[]{:S(2)}) %all-to-all-start.7) | async-done | bytes 131104 | tf_op jit(solution)/shard_map/all_to_all | solution.py:344
  152.3 10.5 %all_to_all.127.pieces_ref = bf16[16,8,128]{2,1,0:T(8,128)(2,1)S(1)} all-to-all(bf16[16,8,128]{2,1,0:T(8,128)(2,1)S(1)} %shard_map.94), channel_id=1, replica_groups=mesh['zlo'=4,'x'=4,'y'=8,'zhi'=2,'core'=2] {'y','core'}, dimensions={0} | all-to-all | bytes 65536 | tf_op jit(solution)/shard_map/all_to_all | solution.py:344
  164.8 6.7 %all_to_all.128.pieces_ref = bf16[4,32,128]{2,1,0:T(8,128)(2,1)S(1)} all-to-all(bf16[4,32,128]{2,1,0:T(8,128)(2,1)S(1)} %shard_map.95), channel_id=1, replica_groups=mesh['zlo'=4,'x'=4,'y'=8,'zhi'=2,'core'=2] {'x'}, dimensions={0} | all-to-all | bytes 65536 | tf_op jit(solution)/shard_map/all_to_all | solution.py:344
  171.6 13.3 %all_to_all.129 = bf16[16,32,128]{2,1,0:T(8,128)(2,1)S(1)} all-to-all(bf16[16,32,128]{2,1,0:T(8,128)(2,1)S(1)} %shard_map.96), channel_id=1, replica_groups=mesh['zlo'=4,'x'=4,'y'=8,'zhi'=2,'core'=2] {'y','core'}, dimensions={0} | all-to-all | bytes 262144 | tf_op jit(solution)/shard_map/all_to_all | solution.py:344
  192.8 14.0 %all_to_all.130.pieces_ref = bf16[64,8,128]{2,1,0:T(8,128)(2,1)S(1)} all-to-all(bf16[64,8,128]{2,1,0:T(8,128)(2,1)S(1)} %bitcast.55), channel_id=1, replica_groups=mesh['zlo'=4,'x'=4,'y'=8,'zhi'=2,'core'=2] {'x','y','core'}, dimensions={0} | all-to-all | bytes 262144 | tf_op jit(solution)/shard_map/all_to_all | solution.py:344
  207.4 10.6 %all_to_all.131.pieces_ref = bf16[16,8,128]{2,1,0:T(8,128)(2,1)S(1)} all-to-all(bf16[16,8,128]{2,1,0:T(8,128)(2,1)S(1)} %shard_map.100), channel_id=1, replica_groups=mesh['zlo'=4,'x'=4,'y'=8,'zhi'=2,'core'=2] {'y','core'}, dimensions={0} | all-to-all | bytes 65536 | tf_op jit(solution)/shard_map/all_to_all | solution.py:344
  220.0 6.7 %all_to_all.132.pieces_ref = bf16[4,32,128]{2,1,0:T(8,128)(2,1)S(1)} all-to-all(bf16[4,32,128]{2,1,0:T(8,128)(2,1)S(1)} %shard_map.101), channel_id=1, replica_groups=mesh['zlo'=4,'x'=4,'y'=8,'zhi'=2,'core'=2] {'x'}, dimensions={0} | all-to-all | bytes 65536 | tf_op jit(solution)/shard_map/all_to_all | solution.py:344
  226.8 13.2 %all_to_all.133 = bf16[16,32,128]{2,1,0:T(8,128)(2,1)S(1)} all-to-all(bf16[16,32,128]{2,1,0:T(8,128)(2,1)S(1)} %shard_map.102), channel_id=1, replica_groups=mesh['zlo'=4,'x'=4,'y'=8,'zhi'=2,'core'=2] {'y','core'}, dimensions={0} | all-to-all | bytes 262144 | tf_op jit(solution)/shard_map/all_to_all | solution.py:344
  245.8 13.9 %all_to_all.134.pieces_ref = bf16[64,8,128]{2,1,0:T(8,128)(2,1)S(1)} all-to-all(bf16[64,8,128]{2,1,0:T(8,128)(2,1)S(1)} %bitcast.65), channel_id=1, replica_groups=mesh['zlo'=4,'x'=4,'y'=8,'zhi'=2,'core'=2] {'x','y','core'}, dimensions={0} | all-to-all | bytes 262144 | tf_op jit(solution)/shard_map/all_to_all | solution.py:344
  260.3 10.6 %all_to_all.135.pieces_ref = bf16[16,8,128]{2,1,0:T(8,128)(2,1)S(1)} all-to-all(bf16[16,8,128]{2,1,0:T(8,128)(2,1)S(1)} %shard_map.109), channel_id=1, replica_groups=mesh['zlo'=4,'x'=4,'y'=8,'zhi'=2,'core'=2] {'y','core'}, dimensions={0} | all-to-all | bytes 65536 | tf_op jit(solution)/shard_map/all_to_all | solution.py:344
  278.0 13.3 %all_to_all.137 = bf16[16,32,128]{2,1,0:T(8,128)(2,1)S(1)} all-to-all(bf16[16,32,128]{2,1,0:T(8,128)(2,1)S(1)} %shard_map.111), channel_id=1, replica_groups=mesh['zlo'=4,'x'=4,'y'=8,'zhi'=2,'core'=2] {'y','core'}, dimensions={0} | all-to-all | bytes 262144 | tf_op jit(solution)/shard_map/all_to_all | solution.py:344
  299.5 13.9 %all_to_all.138.pieces_ref = bf16[64,8,128]{2,1,0:T(8,128)(2,1)S(1)} all-to-all(bf16[64,8,128]{2,1,0:T(8,128)(2,1)S(1)} %bitcast.64), channel_id=1, replica_groups=mesh['zlo'=4,'x'=4,'y'=8,'zhi'=2,'core'=2] {'x','y','core'}, dimensions={0} | all-to-all | bytes 262144 | tf_op jit(solution)/shard_map/all_to_all | solution.py:344
  314.1 10.8 %all_to_all.139.pieces_ref = bf16[16,8,128]{2,1,0:T(8,128)(2,1)S(1)} all-to-all(bf16[16,8,128]{2,1,0:T(8,128)(2,1)S(1)} %shard_map.114), channel_id=1, replica_groups=mesh['zlo'=4,'x'=4,'y'=8,'zhi'=2,'core'=2] {'y','core'}, dimensions={0} | all-to-all | bytes 65536 | tf_op jit(solution)/shard_map/all_to_all | solution.py:344
  331.9 13.3 %all_to_all.141 = bf16[16,32,128]{2,1,0:T(8,128)(2,1)S(1)} all-to-all(bf16[16,32,128]{2,1,0:T(8,128)(2,1)S(1)} %get-tuple-element.31), channel_id=1, replica_groups=mesh['zlo'=4,'x'=4,'y'=8,'zhi'=2,'core'=2] {'y','core'}, dimensions={0} | all-to-all | bytes 262144 | tf_op jit(solution)/shard_map/all_to_all | solution.py:344
  345.4 15.5 %all_to_all.142.pieces_ref = bf16[8,144,128]{2,1,0:T(8,128)(2,1)S(1)} all-to-all(bf16[8,144,128]{2,1,0:T(8,128)(2,1)S(1)} %shard_map.117), channel_id=1, replica_groups=mesh['zlo'=4,'x'=4,'y'=8,'zhi'=2,'core'=2] {'zhi','zlo'}, dimensions={0} | all-to-all | bytes 589824 | tf_op jit(solution)/shard_map/all_to_all | solution.py:344
  (97 shorter events, 70.9 us)
Async XLA Ops:
  7.2 63.8 %all-gather.9.cloned.1.call-start = ((), (), s32[]{:S(2)}) async-start(), calls=%async_computation.24 | async-start | bytes 2359296 | tf_op jit(solution)/shard_map/all_gather | solution.py:356
  7.9 177.2 %all-gather.11.cloned.1.call-start = ((), (), s32[]{:S(2)}) async-start(), calls=%async_computation.25 | async-start | bytes 4718592 | tf_op jit(solution)/shard_map/all_gather | solution.py:394
  8.6 23.2 %copy-start = (bf16[1,4,512,512]{3,2,1,0:T(8,128)(2,1)S(1)}, bf16[1,4,512,512]{3,2,1,0:T(8,128)(2,1)}, u32[]{:S(2)}) copy-start(bf16[1,4,512,512]{3,2,1,0:T(8,128)(2,1)} %param.7) | copy-start | bytes 6291460
  8.6 23.2 %copy-start.1 = (bf16[1,512,2048]{2,1,0:T(8,128)(2,1)S(1)}, bf16[1,512,2048]{2,1,0:T(8,128)(2,1)}, u32[]{:S(2)}) copy-start(bf16[1,512,2048]{2,1,0:T(8,128)(2,1)} %param.8) | copy-start | bytes 6291460
  8.6 23.2 %copy-start.19 = (f32[1,2048]{1,0:T(1,128)S(1)}, f32[1,2048]{1,0:T(1,128)}, u32[]{:S(2)}) copy-start(f32[1,2048]{1,0:T(1,128)} %scale_ref.9) | copy-start | bytes 24580
  13.3 17.9 %copy-start.22 = (bf16[256,192]{1,0:T(8,128)(2,1)}, bf16[256,192]{1,0:T(8,128)(2,1)S(1)}, u32[]{:S(2)}) copy-start(bf16[256,192]{1,0:T(8,128)(2,1)S(1)} %get-tuple-element.23.pack_ref) | copy-start | bytes 294916
  35.5 1.4 copy-start.12
  37.7 67.0 %copy-start.14 = (bf16[1,48,2048]{2,1,0:T(8,128)(2,1)S(1)}, bf16[1,48,2048]{2,1,0:T(8,128)(2,1)}, u32[]{:S(2)}) copy-start(bf16[1,48,2048]{2,1,0:T(8,128)(2,1)} %param.10) | copy-start | bytes 589828
  37.7 202.5 %all-gather.13.cloned.1.call-start = ((), (), s32[]{:S(2)}) async-start(), calls=%async_computation.26 | async-start | bytes 4718592 | tf_op jit(solution)/shard_map/all_gather | solution.py:394
  71.0 33.7 %copy-start.2 = (bf16[1,512,2048]{2,1,0:T(8,128)(2,1)S(1)}, bf16[1,512,2048]{2,1,0:T(8,128)(2,1)}, u32[]{:S(2)}) copy-start(bf16[1,512,2048]{2,1,0:T(8,128)(2,1)} %param.8) | copy-start | bytes 6291460
  71.0 1.7 copy-start.5
  105.6 22.9 %copy-start.13 = (bf16[512,2048]{1,0:T(8,128)(2,1)S(1)}, bf16[512,2048]{1,0:T(8,128)(2,1)}, u32[]{:S(2)}) copy-start(bf16[512,2048]{1,0:T(8,128)(2,1)} %copy-done.12) | copy-start | bytes 6291460
  113.0 14.7 %copy-start.20 = (bf16[48,2048]{1,0:T(8,128)(2,1)}, bf16[48,2048]{1,0:T(8,128)(2,1)S(1)}, u32[]{:S(2)}) copy-start(bf16[48,2048]{1,0:T(8,128)(2,1)S(1)} %get-tuple-element.33.corrected_ref) | copy-start | bytes 589828
  128.5 23.2 %copy-start.15 = (f32[8192]{0:T(1024)S(1)}, f32[8192]{0:T(1024)}, u32[]{:S(2)}) copy-start(f32[8192]{0:T(1024)} %param.12) | copy-start | bytes 98308
  134.2 17.6 %all-to-all-start.7 = ((bf16[64,8,128]{2,1,0:T(8,128)(2,1)}), bf16[64,8,128]{2,1,0:T(8,128)(2,1)S(1)}, u32[]{:S(2)}, u32[]{:S(2)}) async-start(bf16[64,8,128]{2,1,0:T(8,128)(2,1)} %bitcast.12), calls=%async_computation.7 | async-start | bytes 262144 | tf_op jit(solution)/shard_map/all_to_all | solution.py:344
  141.3 150.2 %all-gather.15.cloned.1.call-start = ((), (), s32[]{:S(2)}) async-start(), calls=%async_computation.27 | async-start | bytes 4718592 | tf_op jit(solution)/shard_map/all_gather | solution.py:394
  162.8 1.6 copy-start.6
  185.1 3.0 copy-start.3
  185.1 3.5 copy-start.11
  218.0 1.6 copy-start.7
  242.8 28.1 %copy-start.8 = (bf16[4096,256]{1,0:T(8,128)(2,1)S(1)}, bf16[4096,256]{1,0:T(8,128)(2,1)}, u32[]{:S(2)}) copy-start(bf16[4096,256]{1,0:T(8,128)(2,1)} %all-gather.9.cloned.1.call-done) | copy-start | bytes 6291460
  296.6 28.3 %copy-start.9 = (bf16[4096,256]{1,0:T(8,128)(2,1)S(1)}, bf16[4096,256]{1,0:T(8,128)(2,1)}, u32[]{:S(2)}) copy-start(bf16[4096,256]{1,0:T(8,128)(2,1)} %all-gather.9.cloned.1.call-done) | copy-start | bytes 6291460
  314.0 46.9 %copy-start.4 = (bf16[1,512,2048]{2,1,0:T(8,128)(2,1)S(1)}, bf16[1,512,2048]{2,1,0:T(8,128)(2,1)}, u32[]{:S(2)}) copy-start(bf16[1,512,2048]{2,1,0:T(8,128)(2,1)} %param.8) | copy-start | bytes 6291460
  314.0 46.9 %copy-start.21 = (bf16[48,2048]{1,0:T(8,128)(2,1)S(1)}, bf16[48,2048]{1,0:T(8,128)(2,1)}, u32[]{:S(2)}) copy-start(bf16[48,2048]{1,0:T(8,128)(2,1)} %copy-done.20) | copy-start | bytes 589828
  (6 other events, 5.3 us)
Sparse Core Ops, SparseCore 0:
  10.1 45.3 all-gather.8
  57.5 61.8 all-gather.10
  134.3 50.8 all-gather.12
  192.9 50.4 all-gather.14

commit v3 on v2

--- a/solution.py
+++ b/solution.py
@@ -149,9 +149,23 @@
     copies(out_ref, (side - sum_of(pieces_ref)).astype(BF16))
 
 
-def step_kernel(pieces_ref, inverse_ref, out_ref):
+def fetched_step_kernel(pieces_ref, inverse_hbm, out_ref, inverse_ref, sems):
+    fetches = [
+        pltpu.make_async_copy(inverse_hbm.at[zh], inverse_ref.at[zh], sems.at[zh])
+        for zh in range(2)
+    ]
+    for fetch in fetches:
+        fetch.start()
+    step_kernel(pieces_ref, inverse_ref, out_ref, fetches)
+
+
+def step_kernel(pieces_ref, inverse_ref, out_ref, fetches=()):
     rhs = jnp.concatenate([pieces_ref[m] for m in range(pieces_ref.shape[0])], axis=1)
-    parts = [dot(rhs, inverse_ref[zh]) for zh in range(2)]
+    parts = []
+    for zh in range(2):
+        if fetches:
+            fetches[zh].wait()
+        parts.append(dot(rhs, inverse_ref[zh]))
     parts = [part[:, h * PANEL : (h + 1) * PANEL] for part in parts for h in range(2)]
     copies(out_ref, jnp.concatenate(parts, axis=0).astype(BF16))
 
@@ -229,7 +243,7 @@
             out_ref[zi, rows, :] = pieces[zi * size : (zi + 1) * size]
         return carry
 
-    lax.fori_loop(0, SOLVES - 1, solve, 0)
+    lax.fori_loop(0, SOLVES - 1, solve, 0, unroll=True)
 
 
 def ahead_rows(ahead_ref, k):
@@ -398,7 +412,10 @@
         else:
             pieces, = call(rhs_kernel, [(line, ROWS, PANEL)], where, pieces, step, scales)
         pieces = swap(pieces, LINE)
-        pieces, = call(step_kernel, [(4,) + parts], pieces, inverse)
+        if k < 3:
+            pieces, = call(fetched_step_kernel, [(4,) + parts], pieces, inverse, fetched=(1,))
+        else:
+            pieces, = call(step_kernel, [(4,) + parts], pieces, inverse)
         pieces = swap(pieces, "x")
         if last:
             pieces, own = call(last_total_kernel, [(line,) + parts, parts], pieces)

time: 374 us -> 374 us (level)
  local copies, waits for them, and re-layouts: 12.2 us -> 7.25 us
  Pallas kernels: 51.7 us -> 56.1 us
    unnamed x50 -> x44, local copies, waits for them, and re-layouts: 12.2 us -> 7.25 us
    pallas_call x33, Pallas kernels: 51.7 us -> 56.1 us  [call(): pl.pallas_call(body, out_shape=outs, in_specs=[anywhere if i in fetched e...]
  transfers between devices with their start and end apart: 5 -> 5, of which waited for: 1 -> 1; matrix products, arithmetic and copies ran while one was open for 0% -> 0% of each run, Pallas kernels for 10% -> 11%
where the time goes in v3:
time: 374 us; the launch traced here: 373 us
  blocking collectives  276 us (74%)
  Pallas kernels  56.1 us (15%)
  between operations  14.1 us (4%)
  waiting for transfers between devices  10.9 us (3%)
  starting transfers between devices  8.32 us (2%)
  local copies, waits for them, and re-layouts  7.25 us (2%)
    all_to_all x23, blocking collectives, swap(): return lax.all_to_all(x, axes, 0, 0, tiled=True)  276 us
    pallas_call x33, Pallas kernels, call(): pl.pallas_call(body, out_shape=outs, in_specs=[anywhere if i in fetched e...  56.1 us
    all_to_all x1, waiting for transfers between devices, swap(): return lax.all_to_all(x, axes, 0, 0, tiled=True)  10.1 us
    all_to_all x1, starting transfers between devices, swap(): return lax.all_to_all(x, axes, 0, 0, tiled=True)  8.16 us
  transfers between devices with their start and end apart: 5, of which 1 were waited for; matrix products, arithmetic and copies ran while one was open for 0% of the time, Pallas kernels for 11%

profile of v3, /device:TPU:1, one launch (start us, length us, event | category | flops | bytes accessed | tf_op | source)
XLA Modules:
  0.0 373.0 jit_solution(15172503236372221766)
XLA Ops:
  13.3 17.9 %all_to_all.120 = bf16[8,32,128]{2,1,0:T(8,128)(2,1)S(1)} all-to-all(bf16[8,32,128]{2,1,0:T(8,128)(2,1)S(1)} %bitcast.69), channel_id=1, replica_groups=mesh['zlo'=4,'x'=4,'y'=8,'zhi'=2,'core'=2] {'zhi','zlo'}, dimensions={0} | all-to-all | bytes 131072 | tf_op jit(solution)/shard_map/all_to_all | solution.py:358
  37.8 22.5 %all_to_all.121.pieces_ref = bf16[64,8,128]{2,1,0:T(8,128)(2,1)S(1)} all-to-all(bf16[64,8,128]{2,1,0:T(8,128)(2,1)S(1)} %bitcast.62), channel_id=1, replica_groups=mesh['zlo'=4,'x'=4,'y'=8,'zhi'=2,'core'=2] {'x','y','core'}, dimensions={0} | all-to-all | bytes 262144 | tf_op jit(solution)/shard_map/all_to_all | solution.py:358
  60.3 10.6 %all_to_all.122.pieces_ref = bf16[16,8,128]{2,1,0:T(8,128)(2,1)S(1)} all-to-all(bf16[16,8,128]{2,1,0:T(8,128)(2,1)S(1)} %shard_map.88), channel_id=1, replica_groups=mesh['zlo'=4,'x'=4,'y'=8,'zhi'=2,'core'=2] {'y','core'}, dimensions={0} | all-to-all | bytes 65536 | tf_op jit(solution)/shard_map/all_to_all | solution.py:358
  73.2 6.7 %all_to_all.123.pieces_ref = bf16[4,32,128]{2,1,0:T(8,128)(2,1)S(1)} all-to-all(bf16[4,32,128]{2,1,0:T(8,128)(2,1)S(1)} %shard_map.89), channel_id=1, replica_groups=mesh['zlo'=4,'x'=4,'y'=8,'zhi'=2,'core'=2] {'x'}, dimensions={0} | all-to-all | bytes 65536 | tf_op jit(solution)/shard_map/all_to_all | solution.py:358
  79.9 13.2 %all_to_all.124 = bf16[16,32,128]{2,1,0:T(8,128)(2,1)S(1)} all-to-all(bf16[16,32,128]{2,1,0:T(8,128)(2,1)S(1)} %shard_map.90), channel_id=1, replica_groups=mesh['zlo'=4,'x'=4,'y'=8,'zhi'=2,'core'=2] {'y','core'}, dimensions={0} | all-to-all | bytes 262144 | tf_op jit(solution)/shard_map/all_to_all | solution.py:358
  93.4 11.4 %all_to_all.125 = bf16[8,32,128]{2,1,0:T(8,128)(2,1)S(1)} all-to-all(bf16[8,32,128]{2,1,0:T(8,128)(2,1)S(1)} %bitcast.67), channel_id=1, replica_groups=mesh['zlo'=4,'x'=4,'y'=8,'zhi'=2,'core'=2] {'zhi','zlo'}, dimensions={0} | all-to-all | bytes 131072 | tf_op jit(solution)/shard_map/all_to_all | solution.py:358
  112.2 13.8 %all_to_all.126.ahead_ref.base_ref = bf16[8,128,128]{2,1,0:T(8,128)(2,1)S(1)} all-to-all(bf16[8,128,128]{2,1,0:T(8,128)(2,1)S(1)} %get-tuple-element.24), channel_id=1, replica_groups=mesh['zlo'=4,'x'=4,'y'=8,'zhi'=2,'core'=2] {'zhi','zlo'}, dimensions={0} | all-to-all | bytes 524288 | tf_op jit(solution)/shard_map/all_to_all | solution.py:358
  132.6 8.2 %all-to-all-start.7 = ((bf16[64,8,128]{2,1,0:T(8,128)(2,1)}), bf16[64,8,128]{2,1,0:T(8,128)(2,1)S(1)}, u32[]{:S(2)}, u32[]{:S(2)}) async-start(bf16[64,8,128]{2,1,0:T(8,128)(2,1)} %bitcast.12), calls=%async_computation.7 | async-start | bytes 262144 | tf_op jit(solution)/shard_map/all_to_all | solution.py:358
  140.9 10.1 %all-to-all-done.7.pieces_ref = bf16[64,8,128]{2,1,0:T(8,128)(2,1)S(1)} async-done(((bf16[64,8,128]{2,1,0:T(8,128)(2,1)}), bf16[64,8,128]{2,1,0:T(8,128)(2,1)S(1)}, u32[]{:S(2)}, u32[]{:S(2)}) %all-to-all-start.7) | async-done | bytes 131104 | tf_op jit(solution)/shard_map/all_to_all | solution.py:358
  151.6 10.7 %all_to_all.127.pieces_ref = bf16[16,8,128]{2,1,0:T(8,128)(2,1)S(1)} all-to-all(bf16[16,8,128]{2,1,0:T(8,128)(2,1)S(1)} %shard_map.94), channel_id=1, replica_groups=mesh['zlo'=4,'x'=4,'y'=8,'zhi'=2,'core'=2] {'y','core'}, dimensions={0} | all-to-all | bytes 65536 | tf_op jit(solution)/shard_map/all_to_all | solution.py:358
  164.4 6.8 %all_to_all.128.pieces_ref = bf16[4,32,128]{2,1,0:T(8,128)(2,1)S(1)} all-to-all(bf16[4,32,128]{2,1,0:T(8,128)(2,1)S(1)} %shard_map.95), channel_id=1, replica_groups=mesh['zlo'=4,'x'=4,'y'=8,'zhi'=2,'core'=2] {'x'}, dimensions={0} | all-to-all | bytes 65536 | tf_op jit(solution)/shard_map/all_to_all | solution.py:358
  171.3 13.4 %all_to_all.129 = bf16[16,32,128]{2,1,0:T(8,128)(2,1)S(1)} all-to-all(bf16[16,32,128]{2,1,0:T(8,128)(2,1)S(1)} %shard_map.96), channel_id=1, replica_groups=mesh['zlo'=4,'x'=4,'y'=8,'zhi'=2,'core'=2] {'y','core'}, dimensions={0} | all-to-all | bytes 262144 | tf_op jit(solution)/shard_map/all_to_all | solution.py:358
  192.6 13.9 %all_to_all.130.pieces_ref = bf16[64,8,128]{2,1,0:T(8,128)(2,1)S(1)} all-to-all(bf16[64,8,128]{2,1,0:T(8,128)(2,1)S(1)} %bitcast.55), channel_id=1, replica_groups=mesh['zlo'=4,'x'=4,'y'=8,'zhi'=2,'core'=2] {'x','y','core'}, dimensions={0} | all-to-all | bytes 262144 | tf_op jit(solution)/shard_map/all_to_all | solution.py:358
  207.1 10.6 %all_to_all.131.pieces_ref = bf16[16,8,128]{2,1,0:T(8,128)(2,1)S(1)} all-to-all(bf16[16,8,128]{2,1,0:T(8,128)(2,1)S(1)} %shard_map.100), channel_id=1, replica_groups=mesh['zlo'=4,'x'=4,'y'=8,'zhi'=2,'core'=2] {'y','core'}, dimensions={0} | all-to-all | bytes 65536 | tf_op jit(solution)/shard_map/all_to_all | solution.py:358
  219.9 6.7 %all_to_all.132.pieces_ref = bf16[4,32,128]{2,1,0:T(8,128)(2,1)S(1)} all-to-all(bf16[4,32,128]{2,1,0:T(8,128)(2,1)S(1)} %shard_map.101), channel_id=1, replica_groups=mesh['zlo'=4,'x'=4,'y'=8,'zhi'=2,'core'=2] {'x'}, dimensions={0} | all-to-all | bytes 65536 | tf_op jit(solution)/shard_map/all_to_all | solution.py:358
  226.6 13.2 %all_to_all.133 = bf16[16,32,128]{2,1,0:T(8,128)(2,1)S(1)} all-to-all(bf16[16,32,128]{2,1,0:T(8,128)(2,1)S(1)} %shard_map.102), channel_id=1, replica_groups=mesh['zlo'=4,'x'=4,'y'=8,'zhi'=2,'core'=2] {'y','core'}, dimensions={0} | all-to-all | bytes 262144 | tf_op jit(solution)/shard_map/all_to_all | solution.py:358
  245.6 13.9 %all_to_all.134.pieces_ref = bf16[64,8,128]{2,1,0:T(8,128)(2,1)S(1)} all-to-all(bf16[64,8,128]{2,1,0:T(8,128)(2,1)S(1)} %bitcast.65), channel_id=1, replica_groups=mesh['zlo'=4,'x'=4,'y'=8,'zhi'=2,'core'=2] {'x','y','core'}, dimensions={0} | all-to-all | bytes 262144 | tf_op jit(solution)/shard_map/all_to_all | solution.py:358
  260.2 10.6 %all_to_all.135.pieces_ref = bf16[16,8,128]{2,1,0:T(8,128)(2,1)S(1)} all-to-all(bf16[16,8,128]{2,1,0:T(8,128)(2,1)S(1)} %shard_map.109), channel_id=1, replica_groups=mesh['zlo'=4,'x'=4,'y'=8,'zhi'=2,'core'=2] {'y','core'}, dimensions={0} | all-to-all | bytes 65536 | tf_op jit(solution)/shard_map/all_to_all | solution.py:358
  271.2 6.7 %all_to_all.136.pieces_ref = bf16[4,32,128]{2,1,0:T(8,128)(2,1)S(1)} all-to-all(bf16[4,32,128]{2,1,0:T(8,128)(2,1)S(1)} %shard_map.110), channel_id=1, replica_groups=mesh['zlo'=4,'x'=4,'y'=8,'zhi'=2,'core'=2] {'x'}, dimensions={0} | all-to-all | bytes 65536 | tf_op jit(solution)/shard_map/all_to_all | solution.py:358
  277.9 13.3 %all_to_all.137 = bf16[16,32,128]{2,1,0:T(8,128)(2,1)S(1)} all-to-all(bf16[16,32,128]{2,1,0:T(8,128)(2,1)S(1)} %shard_map.111), channel_id=1, replica_groups=mesh['zlo'=4,'x'=4,'y'=8,'zhi'=2,'core'=2] {'y','core'}, dimensions={0} | all-to-all | bytes 262144 | tf_op jit(solution)/shard_map/all_to_all | solution.py:358
  299.4 13.9 %all_to_all.138.pieces_ref = bf16[64,8,128]{2,1,0:T(8,128)(2,1)S(1)} all-to-all(bf16[64,8,128]{2,1,0:T(8,128)(2,1)S(1)} %bitcast.64), channel_id=1, replica_groups=mesh['zlo'=4,'x'=4,'y'=8,'zhi'=2,'core'=2] {'x','y','core'}, dimensions={0} | all-to-all | bytes 262144 | tf_op jit(solution)/shard_map/all_to_all | solution.py:358
  313.9 10.8 %all_to_all.139.pieces_ref = bf16[16,8,128]{2,1,0:T(8,128)(2,1)S(1)} all-to-all(bf16[16,8,128]{2,1,0:T(8,128)(2,1)S(1)} %shard_map.114), channel_id=1, replica_groups=mesh['zlo'=4,'x'=4,'y'=8,'zhi'=2,'core'=2] {'y','core'}, dimensions={0} | all-to-all | bytes 65536 | tf_op jit(solution)/shard_map/all_to_all | solution.py:358
  331.8 13.3 %all_to_all.141 = bf16[16,32,128]{2,1,0:T(8,128)(2,1)S(1)} all-to-all(bf16[16,32,128]{2,1,0:T(8,128)(2,1)S(1)} %get-tuple-element.31), channel_id=1, replica_groups=mesh['zlo'=4,'x'=4,'y'=8,'zhi'=2,'core'=2] {'y','core'}, dimensions={0} | all-to-all | bytes 262144 | tf_op jit(solution)/shard_map/all_to_all | solution.py:358
  345.3 15.5 %all_to_all.142.pieces_ref = bf16[8,144,128]{2,1,0:T(8,128)(2,1)S(1)} all-to-all(bf16[8,144,128]{2,1,0:T(8,128)(2,1)S(1)} %shard_map.117), channel_id=1, replica_groups=mesh['zlo'=4,'x'=4,'y'=8,'zhi'=2,'core'=2] {'zhi','zlo'}, dimensions={0} | all-to-all | bytes 589824 | tf_op jit(solution)/shard_map/all_to_all | solution.py:358
  (91 shorter events, 71.0 us)
Async XLA Ops:
  7.2 63.8 %all-gather.9.cloned.1.call-start = ((), (), s32[]{:S(2)}) async-start(), calls=%async_computation.24 | async-start | bytes 2359296 | tf_op jit(solution)/shard_map/all_gather | solution.py:370
  7.9 176.9 %all-gather.11.cloned.1.call-start = ((), (), s32[]{:S(2)}) async-start(), calls=%async_computation.25 | async-start | bytes 4718592 | tf_op jit(solution)/shard_map/all_gather | solution.py:408
  8.6 23.2 %copy-start = (bf16[1,4,512,512]{3,2,1,0:T(8,128)(2,1)S(1)}, bf16[1,4,512,512]{3,2,1,0:T(8,128)(2,1)}, u32[]{:S(2)}) copy-start(bf16[1,4,512,512]{3,2,1,0:T(8,128)(2,1)} %param.7) | copy-start | bytes 6291460
  8.6 23.2 %copy-start.1 = (bf16[1,512,2048]{2,1,0:T(8,128)(2,1)S(1)}, bf16[1,512,2048]{2,1,0:T(8,128)(2,1)}, u32[]{:S(2)}) copy-start(bf16[1,512,2048]{2,1,0:T(8,128)(2,1)} %param.8) | copy-start | bytes 6291460
  8.6 23.2 %copy-start.16 = (f32[1,2048]{1,0:T(1,128)S(1)}, f32[1,2048]{1,0:T(1,128)}, u32[]{:S(2)}) copy-start(f32[1,2048]{1,0:T(1,128)} %scale_ref.9) | copy-start | bytes 24580
  13.3 17.9 %copy-start.19 = (bf16[256,192]{1,0:T(8,128)(2,1)}, bf16[256,192]{1,0:T(8,128)(2,1)S(1)}, u32[]{:S(2)}) copy-start(bf16[256,192]{1,0:T(8,128)(2,1)S(1)} %get-tuple-element.23.pack_ref) | copy-start | bytes 294916
  35.5 1.4 copy-start.9
  37.7 67.1 %copy-start.11 = (bf16[1,48,2048]{2,1,0:T(8,128)(2,1)S(1)}, bf16[1,48,2048]{2,1,0:T(8,128)(2,1)}, u32[]{:S(2)}) copy-start(bf16[1,48,2048]{2,1,0:T(8,128)(2,1)} %param.10) | copy-start | bytes 589828
  37.7 202.4 %all-gather.13.cloned.1.call-start = ((), (), s32[]{:S(2)}) async-start(), calls=%async_computation.26 | async-start | bytes 4718592 | tf_op jit(solution)/shard_map/all_gather | solution.py:408
  71.0 33.8 %copy-start.2 = (bf16[1,512,2048]{2,1,0:T(8,128)(2,1)S(1)}, bf16[1,512,2048]{2,1,0:T(8,128)(2,1)}, u32[]{:S(2)}) copy-start(bf16[1,512,2048]{2,1,0:T(8,128)(2,1)} %param.8) | copy-start | bytes 6291460
  104.8 0.9 copy-start.20
  105.7 21.2 %copy-start.10 = (bf16[512,2048]{1,0:T(8,128)(2,1)S(1)}, bf16[512,2048]{1,0:T(8,128)(2,1)}, u32[]{:S(2)}) copy-start(bf16[512,2048]{1,0:T(8,128)(2,1)} %copy-done.9) | copy-start | bytes 6291460
  112.2 13.8 %copy-start.17 = (bf16[48,2048]{1,0:T(8,128)(2,1)}, bf16[48,2048]{1,0:T(8,128)(2,1)S(1)}, u32[]{:S(2)}) copy-start(bf16[48,2048]{1,0:T(8,128)(2,1)S(1)} %get-tuple-element.33.corrected_ref) | copy-start | bytes 589828
  126.9 24.1 %copy-start.12 = (f32[8192]{0:T(1024)S(1)}, f32[8192]{0:T(1024)}, u32[]{:S(2)}) copy-start(f32[8192]{0:T(1024)} %param.12) | copy-start | bytes 98308
  130.4 1.4 copy-start.7
  132.6 18.4 %all-to-all-start.7 = ((bf16[64,8,128]{2,1,0:T(8,128)(2,1)}), bf16[64,8,128]{2,1,0:T(8,128)(2,1)S(1)}, u32[]{:S(2)}, u32[]{:S(2)}) async-start(bf16[64,8,128]{2,1,0:T(8,128)(2,1)} %bitcast.12), calls=%async_computation.7 | async-start | bytes 262144 | tf_op jit(solution)/shard_map/all_to_all | solution.py:358
  140.7 150.7 %all-gather.15.cloned.1.call-start = ((), (), s32[]{:S(2)}) async-start(), calls=%async_computation.27 | async-start | bytes 4718592 | tf_op jit(solution)/shard_map/all_gather | solution.py:408
  184.9 3.0 copy-start.3
  184.9 3.5 copy-start.8
  191.7 0.8 copy-start.15
  242.7 28.1 %copy-start.5 = (bf16[4096,256]{1,0:T(8,128)(2,1)S(1)}, bf16[4096,256]{1,0:T(8,128)(2,1)}, u32[]{:S(2)}) copy-start(bf16[4096,256]{1,0:T(8,128)(2,1)} %all-gather.9.cloned.1.call-done) | copy-start | bytes 6291460
  296.4 28.3 %copy-start.6 = (bf16[4096,256]{1,0:T(8,128)(2,1)S(1)}, bf16[4096,256]{1,0:T(8,128)(2,1)}, u32[]{:S(2)}) copy-start(bf16[4096,256]{1,0:T(8,128)(2,1)} %all-gather.9.cloned.1.call-done) | copy-start | bytes 6291460
  313.9 46.9 %copy-start.4 = (bf16[1,512,2048]{2,1,0:T(8,128)(2,1)S(1)}, bf16[1,512,2048]{2,1,0:T(8,128)(2,1)}, u32[]{:S(2)}) copy-start(bf16[1,512,2048]{2,1,0:T(8,128)(2,1)} %param.8) | copy-start | bytes 6291460
  313.9 46.9 %copy-start.18 = (bf16[48,2048]{1,0:T(8,128)(2,1)S(1)}, bf16[48,2048]{1,0:T(8,128)(2,1)}, u32[]{:S(2)}) copy-start(bf16[48,2048]{1,0:T(8,128)(2,1)} %copy-done.17) | copy-start | bytes 589828
  (3 other events, 2.2 us)
Sparse Core Ops, SparseCore 0:
  10.1 45.3 all-gather.8
  57.5 61.7 all-gather.10
  132.7 51.8 all-gather.12
  192.7 49.9 all-gather.14
